TPU v7x, 32 devices: a whole 2x2x4 slice. The times are simulated.
32 devices in a mesh: dp: 16 (over z, x, core), head: 2 (over y).
Axes of the slice: x: 2, y: 2, z: 4, core: 2. Of those that a mesh axis runs over, the one named last changes fastest.
Arguments:
- tokens: bfloat16 [4, 8192, 768], P(None, 'dp'), may hold values from -6 to 6
- live: int32 [4, 8192], P(None, 'dp'), may hold values from 0 to 1, as said below
- bucket: int32 [4], replicated, may hold values from 64 to 512, as said below
- query_weight: bfloat16 [768, 768], P('dp', 'head'), may hold values from -0.21875 to 0.21875
- key_weight: bfloat16 [768, 768], P('dp', 'head'), may hold values from -0.21875 to 0.21875
- value_weight: bfloat16 [768, 768], P('dp', 'head'), may hold values from -0.21875 to 0.21875
- output_weight: bfloat16 [768, 768], P('head', 'dp'), may hold values from -0.875 to 0.875
- inner_weight: bfloat16 [768, 3072], P('dp', 'head'), may hold values from -0.21875 to 0.21875
- outer_weight: bfloat16 [3072, 768], P('head', 'dp'), may hold values from -0.109375 to 0.109375
- query_bias_vector: bfloat16 [768], P('head'), may hold values from -3 to 3
- value_bias_vector: bfloat16 [768], P('head'), may hold values from -3 to 3
- output_bias_vector: bfloat16 [768], replicated, may hold values from -3 to 3
- inner_bias_vector: bfloat16 [3072], P('head'), may hold values from -3 to 3
- outer_bias_vector: bfloat16 [768], replicated, may hold values from -3 to 3
- first_norm_scale: bfloat16 [768], replicated, may hold values from 0.099609375 to 1.8984375
- first_norm_bias: bfloat16 [768], replicated, may hold values from -2 to 2
- second_norm_scale: bfloat16 [768], replicated, may hold values from 0.099609375 to 1.8984375
- second_norm_bias: bfloat16 [768], replicated, may hold values from -2 to 2
- query_down_matrix: bfloat16 [768, 8], replicated, may hold values from -0.21875 to 0.21875
- value_down_matrix: bfloat16 [768, 8], replicated, may hold values from -0.21875 to 0.21875
- query_up_matrix: float32 [8, 768], P(None, 'head'), may hold values from -1.2 to 1.2
- value_up_matrix: float32 [8, 768], P(None, 'head'), may hold values from -1.2 to 1.2
- cotangent: bfloat16 [4, 8192, 768], P(None, 'dp'), may hold values from -6 to 6
Outputs:
- activations: bfloat16 [4, 8192, 768], P(None, 'dp')
- input_grad: bfloat16 [4, 8192, 768], P(None, 'dp')
- lora_query_grad: float32 [8, 768], P(None, 'head')
- lora_value_grad: float32 [8, 768], P(None, 'head')
Inputs may be any that keep to these rules, and one draw needn't show every extreme that they name: The four micro-batches take the bucket lengths 512, 256, 128 and 64, each once. The slots of micro-batch m form aligned items of bucket[m] slots; live is 1 on a prefix of each item longer than half of it and 0 after.
All inputs are finite; a program needn't handle non-finite values.
Results may differ from a plain program's by a relative error of at most 0.02.
Values may be sent and summed in bfloat16 or wider, within the bound.
No kernel may reach another device: no remote copies, remote signals or barrier semaphores. Data moves between devices by JAX's collectives and lax.ppermute only.
A program may use at most 192 MiB of HBM per device.

v0:
```python
import math

import jax
import jax.numpy as jnp
from jax import lax
from jax.sharding import PartitionSpec as P

HEAD_DIM = 64
ADAPTER_RANK = 8
ALPHA = 16
BUCKET_TOP = 512


eps_norm = 1e-05
masked_score = -1000000000.0
highest = lax.Precision.HIGHEST


def plain_dot(left, right):
    return jnp.dot(left, right, preferred_element_type=jnp.float32)


def back_dot(left, right):
    return lax.dot_general(
        left, right, (((1,), (1,)), ((), ())), preferred_element_type=jnp.float32
    )


def precise_backward(left, right):
    return lax.dot_general(
        left, right, (((1,), (1,)), ((), ())), precision=highest, preferred_element_type=jnp.float32
    )


def norm_rows(rows_in, gain, shift):
    center = rows_in - jnp.mean(rows_in, axis=-1, keepdims=True)
    spread = jnp.mean(center * center, axis=-1, keepdims=True)
    scaled = lax.rsqrt(spread + eps_norm)
    normalized_rows = center * scaled
    return (normalized_rows * gain + shift, normalized_rows, scaled)


def norm_back(grad_in, normalized_rows, scaled, gain):
    weighted = grad_in * gain
    return scaled * (
        weighted
        - jnp.mean(weighted, axis=-1, keepdims=True)
        - normalized_rows * jnp.mean(weighted * normalized_rows, axis=-1, keepdims=True)
    )


def gelu_slope(value_matrix):
    cdf_part = 0.5 * (1.0 + lax.erf(value_matrix / math.sqrt(2.0)))
    pdf_part = jnp.exp(-0.5 * value_matrix * value_matrix) / math.sqrt(2.0 * math.pi)
    return cdf_part + value_matrix * pdf_part


def collect(
    query_weight,
    key_weight,
    value_weight,
    inner_weight,
    output_weight,
    outer_weight,
    inner_bias_vector,
):
    rows_q, rows_k, rows_v, rows_in = (
        lax.all_gather(query_weight, "dp", axis=0, tiled=True),
        lax.all_gather(key_weight, "dp", axis=0, tiled=True),
        lax.all_gather(value_weight, "dp", axis=0, tiled=True),
        lax.all_gather(inner_weight, "dp", axis=0, tiled=True),
    )
    cols_out, cols_ffn = (
        lax.all_gather(output_weight, "dp", axis=1, tiled=True),
        lax.all_gather(outer_weight, "dp", axis=1, tiled=True),
    )
    return (
        rows_q,
        rows_k,
        rows_v,
        rows_in,
        cols_out,
        cols_ffn,
        inner_bias_vector.astype(jnp.float32),
    )


def adapter_gradient_sum(query_gradient, value_gradient):
    return lax.psum((query_gradient, value_gradient), "dp")


def shards(
    tokens,
    live,
    bucket,
    query_weight,
    key_weight,
    value_weight,
    output_weight,
    inner_weight,
    outer_weight,
    query_bias_vector,
    value_bias_vector,
    output_bias_vector,
    inner_bias_vector,
    outer_bias_vector,
    first_norm_scale,
    first_norm_bias,
    second_norm_scale,
    second_norm_bias,
    query_down_matrix,
    value_down_matrix,
    query_up_matrix,
    value_up_matrix,
    cotangent,
):
    micro_count, slots, model_width = tokens.shape
    width = query_weight.shape[1]
    group = width // HEAD_DIM
    blocks = slots // BUCKET_TOP
    adapter_multiplier = ALPHA / ADAPTER_RANK
    inverse = 1.0 / math.sqrt(HEAD_DIM)
    bias_q = query_bias_vector.astype(jnp.float32)
    bias_v = value_bias_vector.astype(jnp.float32)
    bias_out = output_bias_vector.astype(jnp.float32)
    bias_ffn = outer_bias_vector.astype(jnp.float32)
    gain_first = first_norm_scale.astype(jnp.float32)
    shift_first = first_norm_bias.astype(jnp.float32)
    gain_second = second_norm_scale.astype(jnp.float32)
    shift_second = second_norm_bias.astype(jnp.float32)
    down_q32 = query_down_matrix.astype(jnp.float32)
    down_v32 = value_down_matrix.astype(jnp.float32)
    query_total_sum = jnp.zeros(query_up_matrix.shape, jnp.float32)
    value_total_sum = jnp.zeros(value_up_matrix.shape, jnp.float32)
    positions = lax.iota(jnp.int32, BUCKET_TOP)
    outputs = []
    grads = []
    for section in range(micro_count):
        rows_q, rows_k, rows_v, rows_in, cols_out, cols_ffn, bias_in = collect(
            query_weight,
            key_weight,
            value_weight,
            inner_weight,
            output_weight,
            outer_weight,
            inner_bias_vector,
        )
        section_tokens = tokens[section]
        tokens_f32 = section_tokens.astype(jnp.float32)
        section_live = live[section]
        segment = positions // bucket[section]
        same_item = segment[:, None] == segment[None, :]
        live_keys = section_live.reshape(blocks, BUCKET_TOP) == 1
        permitted_mask = (same_item[None, :, :] & live_keys[:, None, :])[:, None, :, :]
        query_down_rows = plain_dot(section_tokens, query_down_matrix).astype(jnp.bfloat16)
        value_down_rows = plain_dot(section_tokens, value_down_matrix).astype(jnp.bfloat16)
        query_matrix = (
            plain_dot(section_tokens, rows_q)
            + bias_q
            + adapter_multiplier
            * jnp.dot(
                query_down_rows.astype(jnp.float32),
                query_up_matrix,
                precision=highest,
                preferred_element_type=jnp.float32,
            )
        )
        value_matrix = (
            plain_dot(section_tokens, rows_v)
            + bias_v
            + adapter_multiplier
            * jnp.dot(
                value_down_rows.astype(jnp.float32),
                value_up_matrix,
                precision=highest,
                preferred_element_type=jnp.float32,
            )
        )
        query_heads = query_matrix.astype(jnp.bfloat16).reshape(blocks, BUCKET_TOP, group, HEAD_DIM)
        key_heads = (
            plain_dot(section_tokens, rows_k)
            .astype(jnp.bfloat16)
            .reshape(blocks, BUCKET_TOP, group, HEAD_DIM)
        )
        value_heads = value_matrix.astype(jnp.bfloat16).reshape(blocks, BUCKET_TOP, group, HEAD_DIM)
        scores = (
            jnp.einsum(
                "nqhd,nkhd->nhqk", query_heads, key_heads, preferred_element_type=jnp.float32
            )
            * inverse
        )
        scores = jnp.where(permitted_mask, scores, masked_score)
        top_score = jnp.max(scores, axis=-1, keepdims=True)
        expo = jnp.exp(scores - top_score)
        probs = expo / jnp.sum(expo, axis=-1, keepdims=True)
        probs_low = probs.astype(jnp.bfloat16)
        context = jnp.einsum(
            "nhqk,nkhd->nqhd", probs_low, value_heads, preferred_element_type=jnp.float32
        )
        context_low = context.reshape(slots, width).astype(jnp.bfloat16)
        attended = lax.psum(plain_dot(context_low, cols_out).astype(jnp.bfloat16), "head").astype(
            jnp.float32
        )
        normed, normal_one, scaled_one = norm_rows(
            tokens_f32 + attended + bias_out, gain_first, shift_first
        )
        normed_low = normed.astype(jnp.bfloat16)
        pre_act = plain_dot(normed_low, rows_in) + bias_in
        activated = jax.nn.gelu(pre_act, approximate=False).astype(jnp.bfloat16)
        fed = lax.psum(plain_dot(activated, cols_ffn).astype(jnp.bfloat16), "head").astype(
            jnp.float32
        )
        out_float, normal_two, scaled_two = norm_rows(
            normed + fed + bias_ffn, gain_second, shift_second
        )
        outputs.append(out_float.astype(jnp.bfloat16))
        grad_out = cotangent[section].astype(jnp.float32) * section_live[:, None].astype(
            jnp.float32
        )
        grad_r_two = norm_back(grad_out, normal_two, scaled_two, gain_second)
        grad_act = back_dot(grad_r_two.astype(jnp.bfloat16), cols_ffn)
        grad_pre = (grad_act * gelu_slope(pre_act)).astype(jnp.bfloat16)
        grad_normed = grad_r_two + lax.psum(
            back_dot(grad_pre, rows_in).astype(jnp.bfloat16), "head"
        ).astype(jnp.float32)
        grad_r_one = norm_back(grad_normed, normal_one, scaled_one, gain_first)
        grad_one_low = grad_r_one.astype(jnp.bfloat16)
        grad_context = back_dot(grad_one_low, cols_out).astype(jnp.bfloat16)
        grad_context = grad_context.reshape(blocks, BUCKET_TOP, group, HEAD_DIM)
        grad_probs = jnp.einsum(
            "nqhd,nkhd->nhqk", grad_context, value_heads, preferred_element_type=jnp.float32
        )
        grad_value = jnp.einsum(
            "nhqk,nqhd->nkhd", probs_low, grad_context, preferred_element_type=jnp.float32
        )
        row_total = jnp.sum(probs * grad_probs, axis=-1, keepdims=True)
        grad_scores = (probs * (grad_probs - row_total)).astype(jnp.bfloat16)
        grad_query = (
            jnp.einsum(
                "nhqk,nkhd->nqhd", grad_scores, key_heads, preferred_element_type=jnp.float32
            )
            * inverse
        )
        grad_key = (
            jnp.einsum(
                "nhqk,nqhd->nkhd", grad_scores, query_heads, preferred_element_type=jnp.float32
            )
            * inverse
        )
        query_gradient_reduced = grad_query.reshape(slots, width).astype(jnp.bfloat16)
        grad_k_low = grad_key.reshape(slots, width).astype(jnp.bfloat16)
        value_gradient_reduced = grad_value.reshape(slots, width).astype(jnp.bfloat16)
        query_down_gradient = adapter_multiplier * precise_backward(
            query_gradient_reduced.astype(jnp.float32), query_up_matrix
        )
        value_down_gradient = adapter_multiplier * precise_backward(
            value_gradient_reduced.astype(jnp.float32), value_up_matrix
        )
        input_part = (
            back_dot(query_gradient_reduced, rows_q)
            + back_dot(grad_k_low, rows_k)
            + back_dot(value_gradient_reduced, rows_v)
        )
        input_part = (
            input_part
            + precise_backward(query_down_gradient, down_q32)
            + precise_backward(value_down_gradient, down_v32)
        )
        grad_tokens = grad_r_one + lax.psum(input_part.astype(jnp.bfloat16), "head").astype(
            jnp.float32
        )
        grads.append(grad_tokens.astype(jnp.bfloat16))
        query_adapter_term = adapter_multiplier * lax.dot_general(
            query_down_rows,
            query_gradient_reduced,
            (((0,), (0,)), ((), ())),
            preferred_element_type=jnp.float32,
        )
        value_adapter_term = adapter_multiplier * lax.dot_general(
            value_down_rows,
            value_gradient_reduced,
            (((0,), (0,)), ((), ())),
            preferred_element_type=jnp.float32,
        )
        query_summed_rows, value_summed_rows = adapter_gradient_sum(
            query_adapter_term, value_adapter_term
        )
        query_total_sum = query_total_sum + query_summed_rows
        value_total_sum = value_total_sum + value_summed_rows
    return (jnp.stack(outputs), jnp.stack(grads), query_total_sum, value_total_sum)


def solution(mesh):
    return jax.shard_map(
        shards,
        mesh=mesh,
        in_specs=(
            P(None, "dp", None),
            P(None, "dp"),
            P(),
            P("dp", "head"),
            P("dp", "head"),
            P("dp", "head"),
            P("head", "dp"),
            P("dp", "head"),
            P("head", "dp"),
            P("head"),
            P("head"),
            P(),
            P("head"),
            P(),
            P(),
            P(),
            P(),
            P(),
            P(),
            P(),
            P(None, "head"),
            P(None, "head"),
            P(None, "dp", None),
        ),
        out_specs=(P(None, "dp", None), P(None, "dp", None), P(None, "head"), P(None, "head")),
        check_vma=False,
    )
```

profile of v0, /device:TPU:0, one launch (start us, length us, event | category | flops | bytes accessed | tf_op | source)
XLA Modules:
  0.0 754.8 jit_solution(17762407008141377688)
XLA Ops:
  14.7 24.8 %all_gather.14 = bf16[768,384]{1,0:T(8,128)(2,1)S(1)} all-gather(bf16[48,384]{1,0:T(8,128)(2,1)S(1)} %copy-done.104), channel_id=1, replica_groups=mesh['dp'=16,'head'=2] {'dp'}, dimensions={0}, use_global_device_ids=true | all-gather | bytes 626688 | tf_op jit(solution)/shard_map/all_gather | solution.py:69
  42.1 19.1 %all_gather.12 = bf16[768,384]{1,0:T(8,128)(2,1)S(1)} all-gather(bf16[48,384]{1,0:T(8,128)(2,1)S(1)} %copy-done.105), channel_id=1, replica_groups=mesh['dp'=16,'head'=2] {'dp'}, dimensions={0}, use_global_device_ids=true | all-gather | bytes 626688 | tf_op jit(solution)/shard_map/all_gather | solution.py:70
  64.1 20.5 %all_gather.13 = bf16[768,384]{1,0:T(8,128)(2,1)S(1)} all-gather(bf16[48,384]{1,0:T(8,128)(2,1)S(1)} %copy-done.106), channel_id=1, replica_groups=mesh['dp'=16,'head'=2] {'dp'}, dimensions={0}, use_global_device_ids=true | all-gather | bytes 626688 | tf_op jit(solution)/shard_map/all_gather | solution.py:68
  94.9 20.6 %all_gather.15 = bf16[384,768]{0,1:T(8,128)(2,1)} all-gather(bf16[384,48]{0,1:T(8,128)(2,1)S(1)} %copy-done.107), channel_id=1, replica_groups=mesh['dp'=16,'head'=2] {'dp'}, dimensions={1}, use_global_device_ids=true | all-gather | bytes 626688 | tf_op jit(solution)/shard_map/all_gather | solution.py:74
  124.3 6.7 fusion.448
  137.4 6.7 fusion.447
  162.9 6.9 fusion.450
  175.0 24.6 %all-reduce.24.cloned.1.call-done = (bf16[512,768]{1,0:T(8,128)(2,1)}, bf16[512,768]{1,0:T(8,128)(2,1)}) async-done(((bf16[512,768]{1,0:T(8,128)(2,1)}, bf16[512,768]{1,0:T(8,128)(2,1)}), (bf16[512,768]{1,0:T(8,128)(2,1)}, bf16[512,768]{1,0:T(8,128)(2,1)})) %all-reduce.24.cloned.1.call-update) | async-done | bytes 1572880 | tf_op jit(solution)/shard_map/psum | solution.py:201
  212.8 24.2 %all-gather.5.cloned.1.call-done = bf16[1536,768]{0,1:T(8,128)(2,1)} async-done(((bf16[1536,48]{0,1:T(8,128)(2,1)}), bf16[1536,768]{0,1:T(8,128)(2,1)}) %all-gather.5.cloned.1.call-update) | async-done | bytes 2359312 | tf_op jit(solution)/shard_map/all_gather | solution.py:75
  237.0 11.2 %fusion.141 = bf16[512,768]{1,0:T(8,128)(2,1)} fusion(bf16[1536,768]{0,1:T(8,128)(2,1)} %all-gather.5.cloned.1.call-done, f32[512,1536]{1,0:T(8,128)} %convolution_add_fusion), kind=kOutput, calls=%fused_computation.257 | convolution fusion | flops 1259470848 | bytes 6291456 | tf_op jit(solution)/shard_map/dot_general | solution.py:20
  248.2 8.8 %fusion.132 = bf16[512,768]{1,0:T(8,128)(2,1)} fusion(bf16[1536,768]{0,1:T(8,128)(2,1)S(1)} %copy-done.159, f32[512,1536]{1,0:T(8,128)S(1)} %copy-done.161), kind=kOutput, calls=%fused_computation.254 | convolution fusion | flops 1259470848 | bytes 6291456 | tf_op jit(solution)/shard_map/dot_general | solution.py:20
  262.6 6.8 fusion.449
  274.6 32.9 %all-reduce.22.cloned.1.call-done = (bf16[512,768]{1,0:T(8,128)(2,1)}, bf16[512,768]{1,0:T(8,128)(2,1)}) async-done(((bf16[512,768]{1,0:T(8,128)(2,1)}, bf16[512,768]{1,0:T(8,128)(2,1)}), (bf16[512,768]{1,0:T(8,128)(2,1)}, bf16[512,768]{1,0:T(8,128)(2,1)})) %all-reduce.22.cloned.1.call-update) | async-done | bytes 1572880 | tf_op jit(solution)/shard_map/psum | solution.py:210
  316.8 7.4 convolution_convert_fusion.3
  324.1 7.4 convolution_convert_fusion
  331.8 86.2 %all-reduce.20.cloned.1.call-done = (bf16[512,768]{1,0:T(8,128)(2,1)}, bf16[512,768]{1,0:T(8,128)(2,1)}, bf16[512,768]{1,0:T(8,128)(2,1)}, bf16[512,768]{1,0:T(8,128)(2,1)}) async-done(((bf16[512,768]{1,0:T(8,128)(2,1)}, bf16[512,768]{1,0:T(8,128)(2,1)}, bf16[512,768]{1,0:T(8,128)(2,1)}, bf16[512,768]{1,0:T(8,128)(2,1)}), (bf16[512,768]{1,0:T(8,128)(2,1)}, bf16[512,768]{1,0:T(8,128)(2,1)}, ...) | async-done | bytes 3145744 | tf_op jit(solution)/shard_map/psum | solution.py:201
  425.9 8.8 %fusion.138 = bf16[512,768]{1,0:T(8,128)(2,1)} fusion(bf16[1536,768]{0,1:T(8,128)(2,1)S(1)} %copy-done.160, f32[512,1536]{1,0:T(8,128)S(1)} %convolution_add_fusion.1), kind=kOutput, calls=%fused_computation.256 | convolution fusion | flops 1259470848 | bytes 6291456 | tf_op jit(solution)/shard_map/dot_general | solution.py:20
  437.9 9.2 %fusion.135 = bf16[512,768]{1,0:T(8,128)(2,1)} fusion(bf16[1536,768]{0,1:T(8,128)(2,1)S(1)} %copy-done.160, f32[512,1536]{1,0:T(8,128)S(1)} %convolution_add_fusion.2), kind=kOutput, calls=%fused_computation.255 | convolution fusion | flops 1259470848 | bytes 6291456 | tf_op jit(solution)/shard_map/dot_general | solution.py:20
  447.2 51.8 %all-reduce.18.cloned.1.call-done = (bf16[512,768]{1,0:T(8,128)(2,1)}, bf16[512,768]{1,0:T(8,128)(2,1)}) async-done(((bf16[512,768]{1,0:T(8,128)(2,1)}, bf16[512,768]{1,0:T(8,128)(2,1)}), (bf16[512,768]{1,0:T(8,128)(2,1)}, bf16[512,768]{1,0:T(8,128)(2,1)})) %all-reduce.18.cloned.1.call-update) | async-done | bytes 1572880 | tf_op jit(solution)/shard_map/psum | solution.py:210
  508.2 7.4 convolution_convert_fusion.2
  515.6 7.4 convolution_convert_fusion.1
  524.2 50.6 %all-reduce.16.cloned.1.call-done = (bf16[512,768]{1,0:T(8,128)(2,1)}, bf16[512,768]{1,0:T(8,128)(2,1)}) async-done(((bf16[512,768]{1,0:T(8,128)(2,1)}, bf16[512,768]{1,0:T(8,128)(2,1)}), (bf16[512,768]{1,0:T(8,128)(2,1)}, bf16[512,768]{1,0:T(8,128)(2,1)})) %all-reduce.16.cloned.1.call-update) | async-done | bytes 1572880 | tf_op jit(solution)/shard_map/psum | solution.py:223
  661.5 61.2 %all-reduce = (f32[8,384]{1,0:T(8,128)}, f32[8,384]{1,0:T(8,128)}) all-reduce(f32[8,384]{1,0:T(8,128)S(1)} %fusion.201, f32[8,384]{1,0:T(8,128)S(1)} %fusion.200), channel_id=1, replica_groups=mesh['dp'=16,'head'=2] {'dp'}, use_global_device_ids=true, to_apply=%region_60.61 | all-reduce | flops 6144 | bytes 49152 | tf_op jit(solution)/shard_map/psum | solution.py:89
  722.7 18.7 %all-reduce.14.cloned.1.call-done = (bf16[512,768]{1,0:T(8,128)(2,1)}, bf16[512,768]{1,0:T(8,128)(2,1)}, bf16[512,768]{1,0:T(8,128)(2,1)}, bf16[512,768]{1,0:T(8,128)(2,1)}) async-done(((bf16[512,768]{1,0:T(8,128)(2,1)}, bf16[512,768]{1,0:T(8,128)(2,1)}, bf16[512,768]{1,0:T(8,128)(2,1)}, bf16[512,768]{1,0:T(8,128)(2,1)}), (bf16[512,768]{1,0:T(8,128)(2,1)}, bf16[512,768]{1,0:T(8,128)(2,1)}, ...) | async-done | bytes 3145744 | tf_op jit(solution)/shard_map/psum | solution.py:269
  (539 shorter events, 204.5 us)
Async XLA Ops:
  8.0 191.5 %all-reduce.24.cloned.1.call-start = ((), (), s32[]{:S(2)}) async-start(), calls=%async_computation.7 | async-start | bytes 3145728 | tf_op jit(solution)/shard_map/psum | solution.py:201
  9.7 110.7 %copy-start.111 = (bf16[512,8]{0,1:T(8,128)(2,1)}, bf16[512,8]{0,1:T(8,128)(2,1)S(1)}, u32[]{:S(2)}) copy-start(bf16[512,8]{0,1:T(8,128)(2,1)S(1)} %convolution_convert_fusion.16) | copy-start | bytes 24580
  13.2 102.3 %copy-start.113 = (bf16[512,8]{0,1:T(8,128)(2,1)}, bf16[512,8]{0,1:T(8,128)(2,1)S(1)}, u32[]{:S(2)}) copy-start(bf16[512,8]{0,1:T(8,128)(2,1)S(1)} %convolution_convert_fusion.17) | copy-start | bytes 24580
  14.7 103.3 %copy-start.109 = (bf16[512,8]{0,1:T(8,128)(2,1)}, bf16[512,8]{0,1:T(8,128)(2,1)S(1)}, u32[]{:S(2)}) copy-start(bf16[512,8]{0,1:T(8,128)(2,1)S(1)} %convolution_convert_fusion.23) | copy-start | bytes 24580
  42.1 43.8 %copy-start.149 = (f32[384]{0:T(512)}, f32[384]{0:T(512)S(1)}, u32[]{:S(2)}) copy-start(f32[384]{0:T(512)S(1)} %convert_element_type.605) | copy-start | bytes 4612
  64.1 51.5 %copy-start.76 = (f32[8,384]{1,0:T(8,128)S(1)}, f32[8,384]{1,0:T(8,128)}, u32[]{:S(2)}) copy-start(f32[8,384]{1,0:T(8,128)} %param.44) | copy-start | bytes 36868
  149.1 54.7 %all-gather.3.cloned.1.call-start = ((), (), s32[]{:S(2)}) async-start(), calls=%async_computation | async-start | bytes 2506752 | tf_op jit(solution)/shard_map/all_gather | solution.py:71
  149.7 87.3 %all-gather.5.cloned.1.call-start = ((), (), s32[]{:S(2)}) async-start(), calls=%async_computation.1 | async-start | bytes 2506752 | tf_op jit(solution)/shard_map/all_gather | solution.py:75
  150.3 157.1 %all-reduce.22.cloned.1.call-start = ((), (), s32[]{:S(2)}) async-start(), calls=%async_computation.6 | async-start | bytes 3145728 | tf_op jit(solution)/shard_map/psum | solution.py:210
  257.1 161.0 %all-reduce.20.cloned.1.call-start = ((), (), s32[]{:S(2)}) async-start(), calls=%async_computation.5 | async-start | bytes 6291456 | tf_op jit(solution)/shard_map/psum | solution.py:201
  269.4 38.0 %copy-start.94 = (f32[512]{0:T(512)S(1)}, f32[512]{0:T(512)}, u32[]{:S(2)}) copy-start(f32[512]{0:T(512)} %copy-done.93) | copy-start | bytes 6148
  269.4 38.0 %copy-start.98 = (f32[512]{0:T(512)S(1)}, f32[512]{0:T(512)}, u32[]{:S(2)}) copy-start(f32[512]{0:T(512)} %copy-done.97) | copy-start | bytes 6148
  269.4 38.0 %copy-start.102 = (f32[768]{0:T(1024)S(1)}, f32[768]{0:T(1024)}, u32[]{:S(2)}) copy-start(f32[768]{0:T(1024)} %convert_element_type.621) | copy-start | bytes 9220
  269.4 38.0 %copy-start.103 = (f32[768]{0:T(1024)S(1)}, f32[768]{0:T(1024)}, u32[]{:S(2)}) copy-start(f32[768]{0:T(1024)} %convert_element_type.627) | copy-start | bytes 9220
  269.4 38.0 %copy-start.125 = (f32[512]{0:T(512)S(1)}, f32[512]{0:T(512)}, u32[]{:S(2)}) copy-start(f32[512]{0:T(512)} %copy-done.124) | copy-start | bytes 6148
  269.4 38.0 %copy-start.128 = (f32[512]{0:T(512)S(1)}, f32[512]{0:T(512)}, u32[]{:S(2)}) copy-start(f32[512]{0:T(512)} %copy-done.127) | copy-start | bytes 6148
  331.6 167.4 %all-reduce.18.cloned.1.call-start = ((), (), s32[]{:S(2)}) async-start(), calls=%async_computation.4 | async-start | bytes 3145728 | tf_op jit(solution)/shard_map/psum | solution.py:210
  422.5 152.3 %copy-start.95 = (f32[512]{0:T(512)}, f32[512]{0:T(512)S(1)}, u32[]{:S(2)}) copy-start(f32[512]{0:T(512)S(1)} %broadcast_multiply_fusion.21) | copy-start | bytes 6148
  423.5 151.4 %copy-start.129 = (f32[512]{0:T(512)}, f32[512]{0:T(512)S(1)}, u32[]{:S(2)}) copy-start(f32[512]{0:T(512)S(1)} %add_rsqrt_fusion.5) | copy-start | bytes 6148
  447.1 127.7 %all-reduce.16.cloned.1.call-start = ((), (), s32[]{:S(2)}) async-start(), calls=%async_computation.3 | async-start | bytes 3145728 | tf_op jit(solution)/shard_map/psum | solution.py:223
  523.0 218.3 %all-reduce.14.cloned.1.call-start = ((), (), s32[]{:S(2)}) async-start(), calls=%async_computation.2 | async-start | bytes 6291456 | tf_op jit(solution)/shard_map/psum | solution.py:269
  584.1 64.3 %copy-start.45 = (bf16[6,64,512]{2,1,0:T(8,128)(2,1)}, bf16[6,64,512]{2,1,0:T(8,128)(2,1)S(1)}, u32[]{:S(2)}) copy-start(bf16[6,64,512]{2,1,0:T(8,128)(2,1)S(1)} %fusion.193) | copy-start | bytes 1179652
  597.7 52.3 %copy-start.47 = (bf16[6,64,512]{2,1,0:T(8,128)(2,1)}, bf16[6,64,512]{2,1,0:T(8,128)(2,1)S(1)}, u32[]{:S(2)}) copy-start(bf16[6,64,512]{2,1,0:T(8,128)(2,1)S(1)} %fusion.187) | copy-start | bytes 1179652
  659.5 81.9 %copy-start.30 = (f32[512,768]{1,0:T(8,128)S(1)}, f32[512,768]{1,0:T(8,128)}, u32[]{:S(2)}) copy-start(f32[512,768]{1,0:T(8,128)} %copy-done.29) | copy-start | bytes 4718596
  (156 other events, 1048.0 us)
Sparse Core Ops, SparseCore 0:
  149.2 50.2 all-reduce.23
  257.2 50.1 all-reduce.21
  331.7 86.3 all-reduce.19
  447.2 51.6 all-reduce.17
  523.2 51.6 all-reduce.15
  655.0 86.3 all-reduce.13
Sparse Core Ops, SparseCore 1:
  152.2 41.3 all-gather.2
  195.9 41.1 all-gather.4
where the time goes:
time: 760 us; the launch traced here: 755 us
  waiting for transfers between devices  290 us (38%)
  matrix products  215 us (28%)
  blocking collectives  146 us (19%)
  other arithmetic  73.9 us (10%)
  between operations  20.5 us (3%)
  local copies, waits for them, and re-layouts  8.33 us (1%)
    psum x2, waiting for transfers between devices, shards(): lax.psum(plain_dot(context_low, cols_out).astype(jnp.bfloat16), 'head')  111 us
    psum x2, waiting for transfers between devices, shards(): lax.psum(plain_dot(activated, cols_ffn).astype(jnp.bfloat16), 'head')  84.6 us
    dot_general x32, matrix products, plain_dot(): return jnp.dot(left, right, preferred_element_type=jnp.float32)  76.8 us
    psum x1, blocking collectives, adapter_gradient_sum(): return lax.psum((query_gradient, value_gradient), 'dp')  61.2 us
    psum x1, waiting for transfers between devices, shards(): lax.psum(back_dot(grad_pre, rows_in).astype(jnp.bfloat16), 'head')  50.6 us
    dot_general x20, matrix products, back_dot(): lax.dot_general(left, right, (((1,), (1,)), ((), ())), preferred_element_...  42.8 us
    sub x4, matrix products, shards(): expo = jnp.exp(scores - top_score)  27.1 us
    all_gather x1, blocking collectives, collect(): lax.all_gather(key_weight, 'dp', axis=0, tiled=True)  24.8 us
  transfers between devices with their start and end apart: 8, of which 7 were waited for; matrix products, arithmetic and copies ran while one was open for 8% of the time, Pallas kernels for 0%

commit v1 on v0

v1 whole, which is shorter than its diff:
```python
import functools
import math
import jax
import jax.numpy as jnp
from jax import lax
from jax.experimental import pallas as pl
from jax.experimental.pallas import tpu as pltpu
from jax.sharding import PartitionSpec as P

F32, BF16 = jnp.float32, jnp.bfloat16
ALPHA = 16
EPS = 1e-5
MASKED = -1e9
NT = (((1,), (1,)), ((), ()))
TN = (((0,), (0,)), ((), ()))
NN = (((1,), (0,)), ((), ()))


def mm(a, b, dims=NN):
    return lax.dot_general(a, b, dims, preferred_element_type=F32)


def lane_masks():
    lane = lax.broadcasted_iota(jnp.int32, (1, 128), 1)
    one, zero = jnp.ones((1, 128), F32), jnp.zeros((1, 128), F32)
    low = jnp.where(lane < 64, one, zero)
    return low.astype(BF16), (one - low).astype(BF16)


def fwd_kernel(ids, bucket, x_ref, w_ref, addq_ref, addv_ref, live_ref, qkv_ref, p_ref, ctx_ref, bias):
    slots, width = x_ref.shape[1], ctx_ref.shape[2]
    span = bucket[ids[pl.program_id(0)]]

    @pl.when(pl.program_id(1) == 0)
    def _():
        t = lax.broadcasted_iota(jnp.int32, (slots, slots), 0)
        s = lax.broadcasted_iota(jnp.int32, (slots, slots), 1)
        ok = ((t ^ s) < span) & (live_ref[0] == 1)
        bias[...] = jnp.where(ok, 0.0, MASKED)

    x = x_ref[0]
    qkv_ref[0, 0, :, :width] = (mm(x, w_ref[0, :, :width]) + addq_ref[0, 0]).astype(BF16)
    qkv_ref[0, 0, :, width : 2 * width] = mm(x, w_ref[0, :, width : 2 * width]).astype(BF16)
    qkv_ref[0, 0, :, 2 * width :] = (mm(x, w_ref[0, :, 2 * width :]) + addv_ref[0, 0]).astype(BF16)
    masks = lane_masks()

    def attend(size):
        def pair(j, _):
            col = pl.multiple_of(j * 128, 128)
            for b in range(slots // size):
                rows = slice(b * size, (b + 1) * size)
                q2 = qkv_ref[0, 0, rows, pl.ds(col, 128)]
                k2 = qkv_ref[0, 0, rows, pl.ds(width + col, 128)] * jnp.asarray(0.125, BF16)
                v2 = qkv_ref[0, 0, rows, pl.ds(2 * width + col, 128)]
                acc = None
                for e in range(2):
                    s = mm(q2, k2 * masks[e], NT) + bias[rows, rows]
                    s = jnp.exp(s - jnp.max(s, axis=1, keepdims=True))
                    probs = (s * (1.0 / jnp.sum(s, axis=1, keepdims=True))).astype(BF16)
                    p_ref[0, 0, 2 * j + e, rows, :size] = probs
                    part = mm(probs, v2 * masks[e])
                    acc = part if acc is None else acc + part
                ctx_ref[0, rows, pl.ds(col, 128)] = acc.astype(BF16)
            return 0

        lax.fori_loop(0, width // 128, pair, 0)

    @pl.when(span == slots)
    def _():
        attend(slots)

    @pl.when(span != slots)
    def _():
        attend(slots // 2)


def run_fwd(ids, bucket, tokens, wqkv, addq, addv, live):
    n = ids.shape[0]
    _, slots, model = tokens.shape
    half = wqkv.shape[2] // 3
    heads = half // 64
    return pl.pallas_call(
        fwd_kernel,
        out_shape=(
            jax.ShapeDtypeStruct((n, 2, slots, 3 * half), BF16),
            jax.ShapeDtypeStruct((n, 2, heads, slots, slots), BF16),
            jax.ShapeDtypeStruct((n, slots, 2 * half), BF16),
        ),
        grid_spec=pltpu.PrefetchScalarGridSpec(
            num_scalar_prefetch=2,
            grid=(n, 2),
            in_specs=[
                pl.BlockSpec((1, slots, model), lambda i, h, ids, b: (ids[i], 0, 0)),
                pl.BlockSpec((1, model, 3 * half), lambda i, h, ids, b: (h, 0, 0)),
                pl.BlockSpec((1, 1, slots, half), lambda i, h, ids, b: (ids[i], h, 0, 0)),
                pl.BlockSpec((1, 1, slots, half), lambda i, h, ids, b: (ids[i], h, 0, 0)),
                pl.BlockSpec((1, 1, slots), lambda i, h, ids, b: (ids[i], 0, 0)),
            ],
            out_specs=[
                pl.BlockSpec((1, 1, slots, 3 * half), lambda i, h, ids, b: (i, h, 0, 0)),
                pl.BlockSpec((1, 1, heads, slots, slots), lambda i, h, ids, b: (i, h, 0, 0, 0)),
                pl.BlockSpec((1, slots, half), lambda i, h, ids, b: (i, 0, h)),
            ],
            scratch_shapes=[pltpu.VMEM((slots, slots), F32)],
        ),
        compiler_params=pltpu.CompilerParams(vmem_limit_bytes=50 << 20),
        name="attention_forward",
    )(ids, bucket, tokens, wqkv, addq, addv, live.reshape(live.shape[0], 1, slots))


RSQRT2 = 1.0 / math.sqrt(2.0)
PHI0 = 1.0 / math.sqrt(2.0 * math.pi)


def gelu_parts(u):
    cdf = 0.5 * (1.0 + lax.erf(u * RSQRT2))
    pdf = jnp.exp(-0.5 * u * u) * PHI0
    return u * cdf, cdf + u * pdf


def norm(rows):
    c = rows - jnp.mean(rows, axis=1, keepdims=True)
    rstd = lax.rsqrt(jnp.mean(c * c, axis=1, keepdims=True) + EPS)
    return c * rstd, rstd


def norm_back(e, xhat, rstd):
    return rstd * (
        e - jnp.mean(e, axis=1, keepdims=True) - xhat * jnp.mean(e * xhat, axis=1, keepdims=True)
    )


def mid_kernel(
    ids, x_ref, ctx_ref, cot_ref, live_ref, wo_ref, wi_ref, wt_ref, bi_ref, vec_ref,
    act_ref, g1_ref, gctx_ref, slope, xhat, acc, low,
):
    slots, model = x_ref.shape[1], x_ref.shape[2]
    half, hid = wo_ref.shape[2], wi_ref.shape[2]
    step = 512
    bo, b2 = vec_ref[0:1], vec_ref[1:2]
    s1, t1, s2, t2 = vec_ref[2:3], vec_ref[3:4], vec_ref[4:5], vec_ref[5:6]
    r1 = x_ref[0].astype(F32) + bo
    for h in range(2):
        r1 = r1 + mm(ctx_ref[0, :, h * half : (h + 1) * half], wo_ref[h], NT)
    xh, rstd1 = norm(r1)
    xhat[...] = xh
    normed = xh * s1 + t1
    low[...] = normed.astype(BF16)
    acc[...] = normed + b2
    for h in range(2):

        def up(j, _):
            cols = pl.ds(pl.multiple_of(j * step, step), step)
            u = mm(low[...], wi_ref[h, :, cols]) + bi_ref[h, :, cols]
            a, d = gelu_parts(u)
            slope[h, :, cols] = d
            acc[...] += mm(a.astype(BF16), wt_ref[h, :, cols], NT)
            return 0

        lax.fori_loop(0, hid // step, up, 0)
    xh2, rstd2 = norm(acc[...])
    act_ref[0] = (xh2 * s2 + t2).astype(BF16)
    e = cot_ref[0].astype(F32) * live_ref[0].astype(F32) * s2
    g2 = norm_back(e, xh2, rstd2)
    low[...] = g2.astype(BF16)
    acc[...] = g2
    for h in range(2):

        def down(j, _):
            cols = pl.ds(pl.multiple_of(j * step, step), step)
            g = mm(low[...], wt_ref[h, :, cols]) * slope[h, :, cols]
            acc[...] += mm(g.astype(BF16), wi_ref[h, :, cols], NT)
            return 0

        lax.fori_loop(0, hid // step, down, 0)
    g1 = norm_back(acc[...] * s1, xhat[...], rstd1)
    g1_ref[0] = g1
    g1 = g1.astype(BF16)
    for h in range(2):
        gctx_ref[0, :, h * half : (h + 1) * half] = mm(g1, wo_ref[h]).astype(BF16)


def run_mid(ids, tokens, ctx, cot, live, wo, wi, wt, bi, vec):
    n = ids.shape[0]
    _, slots, model = tokens.shape
    half, hid = wo.shape[2], wi.shape[2]
    one = pl.Buffered(1)
    return pl.pallas_call(
        mid_kernel,
        out_shape=(
            jax.ShapeDtypeStruct((n, slots, model), BF16),
            jax.ShapeDtypeStruct((n, slots, model), F32),
            jax.ShapeDtypeStruct((n, slots, model), BF16),
        ),
        grid_spec=pltpu.PrefetchScalarGridSpec(
            num_scalar_prefetch=1,
            grid=(n,),
            in_specs=[
                pl.BlockSpec((1, slots, model), lambda i, ids: (ids[i], 0, 0)),
                pl.BlockSpec((1, slots, model), lambda i, ids: (i, 0, 0)),
                pl.BlockSpec((1, slots, model), lambda i, ids: (ids[i], 0, 0)),
                pl.BlockSpec((1, slots, 1), lambda i, ids: (ids[i], 0, 0)),
                pl.BlockSpec((2, model, half), lambda i, ids: (0, 0, 0), pipeline_mode=one),
                pl.BlockSpec((2, model, hid), lambda i, ids: (0, 0, 0), pipeline_mode=one),
                pl.BlockSpec((2, model, hid), lambda i, ids: (0, 0, 0), pipeline_mode=one),
                pl.BlockSpec((2, 1, hid), lambda i, ids: (0, 0, 0), pipeline_mode=one),
                pl.BlockSpec((8, model), lambda i, ids: (0, 0), pipeline_mode=one),
            ],
            out_specs=[
                pl.BlockSpec((1, slots, model), lambda i, ids: (i, 0, 0)),
                pl.BlockSpec((1, slots, model), lambda i, ids: (i, 0, 0)),
                pl.BlockSpec((1, slots, model), lambda i, ids: (i, 0, 0)),
            ],
            scratch_shapes=[
                pltpu.VMEM((2, slots, hid), F32),
                pltpu.VMEM((slots, model), F32),
                pltpu.VMEM((slots, model), F32),
                pltpu.VMEM((slots, model), BF16),
            ],
        ),
        compiler_params=pltpu.CompilerParams(vmem_limit_bytes=58 << 20),
        name="feed_forward",
    )(ids, tokens, ctx, cot, live.reshape(live.shape[0], slots, 1), wo, wi, wt, bi, vec)


def bwd_kernel(
    ids, bucket, qkv_ref, p_ref, gctx_ref, g1_ref, w_ref, zt_ref, u_ref, d_ref,
    grad_ref, lora_ref, dqkv, total, tlo,
):
    slots, width = gctx_ref.shape[1], gctx_ref.shape[2]
    i, h = pl.program_id(0), pl.program_id(1)
    span = bucket[ids[i]]
    masks = lane_masks()

    def attend(size):
        def pair(j, _):
            col = pl.multiple_of(j * 128, 128)
            for b in range(slots // size):
                rows = slice(b * size, (b + 1) * size)
                q2 = qkv_ref[0, 0, rows, pl.ds(col, 128)] * jnp.asarray(0.125, BF16)
                k2 = qkv_ref[0, 0, rows, pl.ds(width + col, 128)] * jnp.asarray(0.125, BF16)
                v2 = qkv_ref[0, 0, rows, pl.ds(2 * width + col, 128)]
                g2 = gctx_ref[0, rows, pl.ds(col, 128)]
                dq = dk = dv = jnp.zeros((size, 128), F32)
                for e in range(2):
                    probs = p_ref[0, 0, 2 * j + e, rows, :size]
                    dp = mm(g2, v2 * masks[e], NT)
                    dv = dv + mm(probs, g2 * masks[e], TN)
                    p32 = probs.astype(F32)
                    pd = p32 * dp
                    ds = (pd - p32 * jnp.sum(pd, axis=1, keepdims=True)).astype(BF16)
                    dq = dq + mm(ds, k2 * masks[e])
                    dk = dk + mm(ds, q2 * masks[e], TN)
                dqkv[rows, pl.ds(col, 128)] = dq.astype(BF16)
                dqkv[rows, pl.ds(width + col, 128)] = dk.astype(BF16)
                dqkv[rows, pl.ds(2 * width + col, 128)] = dv.astype(BF16)
            return 0

        lax.fori_loop(0, width // 128, pair, 0)

    @pl.when(span == slots)
    def _():
        attend(slots)

    @pl.when(span != slots)
    def _():
        attend(slots // 2)

    part = mm(dqkv[...], w_ref[0], NT)
    tq = mm(dqkv[:, :width], u_ref[0, :16], NT)
    tv = mm(dqkv[:, 2 * width :], u_ref[0, 16:], NT)
    t = jnp.concatenate([tq[:, :8] + tq[:, 8:], tv[:, :8] + tv[:, 8:]], axis=1)
    t_high = t.astype(BF16)
    t_low = (t - t_high.astype(F32)).astype(BF16)
    part = part + mm(jnp.concatenate([t_high, t_low], axis=1), d_ref[...])
    lora_ref[0, 0] = 2.0 * mm(zt_ref[0], dqkv[...])

    @pl.when(h == 0)
    def _():
        total[...] = g1_ref[0] + part

    @pl.when(h == 1)
    def _():
        grad_ref[0] = (total[...] + part).astype(BF16)


def run_bwd(ids, bucket, qkv, probs, gctx, g1, wqkv, zt, up, down):
    n, _, slots, width3 = qkv.shape
    half, model = width3 // 3, g1.shape[2]
    heads = half // 64
    return pl.pallas_call(
        bwd_kernel,
        out_shape=(
            jax.ShapeDtypeStruct((n, slots, model), BF16),
            jax.ShapeDtypeStruct((n, 2, 16, width3), F32),
        ),
        grid_spec=pltpu.PrefetchScalarGridSpec(
            num_scalar_prefetch=2,
            grid=(n, 2),
            in_specs=[
                pl.BlockSpec((1, 1, slots, width3), lambda i, h, ids, b: (i, h, 0, 0)),
                pl.BlockSpec((1, 1, heads, slots, slots), lambda i, h, ids, b: (i, h, 0, 0, 0)),
                pl.BlockSpec((1, slots, half), lambda i, h, ids, b: (i, 0, h)),
                pl.BlockSpec((1, slots, model), lambda i, h, ids, b: (i, 0, 0)),
                pl.BlockSpec((1, model, width3), lambda i, h, ids, b: (h, 0, 0)),
                pl.BlockSpec((1, 16, slots), lambda i, h, ids, b: (ids[i], 0, 0)),
                pl.BlockSpec((1, 32, half), lambda i, h, ids, b: (h, 0, 0)),
                pl.BlockSpec((32, model), lambda i, h, ids, b: (0, 0)),
            ],
            out_specs=[
                pl.BlockSpec((1, slots, model), lambda i, h, ids, b: (i, 0, 0)),
                pl.BlockSpec((1, 1, 16, width3), lambda i, h, ids, b: (i, h, 0, 0)),
            ],
            scratch_shapes=[
                pltpu.VMEM((slots, width3), BF16),
                pltpu.VMEM((slots, model), F32),
                pltpu.VMEM((8, 128), F32),
            ],
        ),
        compiler_params=pltpu.CompilerParams(vmem_limit_bytes=50 << 20),
        name="attention_backward",
    )(ids, bucket, qkv, probs, gctx, g1, wqkv, zt, up, down)


def place_kernel(ids, own_ref, peer_ref, out_ref, sems):
    count = own_ref.shape[0]
    copies = [
        pltpu.make_async_copy(ref.at[i], out_ref.at[ids[k * count + i]], sems.at[k * count + i])
        for k, ref in enumerate((own_ref, peer_ref))
        for i in range(count)
    ]
    for copy in copies:
        copy.start()
    for copy in copies:
        copy.wait()


def place(ids, own, peer):
    count, slots, model = own.shape
    return pl.pallas_call(
        place_kernel,
        out_shape=jax.ShapeDtypeStruct((2 * count, slots, model), own.dtype),
        grid_spec=pltpu.PrefetchScalarGridSpec(
            num_scalar_prefetch=1,
            grid=(),
            in_specs=[pl.BlockSpec(memory_space=pl.ANY)] * 2,
            out_specs=pl.BlockSpec(memory_space=pl.ANY),
            scratch_shapes=[pltpu.SemaphoreType.DMA((2 * count,))],
        ),
        name="place",
    )(ids, own, peer)


SWAP = [(0, 1), (1, 0)]


def shards(
    tokens, live, bucket, query_weight, key_weight, value_weight, output_weight, inner_weight,
    outer_weight, query_bias, value_bias, output_bias, inner_bias, outer_bias, first_scale,
    first_bias, second_scale, second_bias, query_down, value_down, query_up, value_up, cotangent,
):
    micro, slots, model = tokens.shape
    half, hid = query_weight.shape[1], inner_weight.shape[1]
    rank = query_up.shape[0]
    scale = ALPHA / rank
    me = lax.axis_index("head")

    packed = jnp.concatenate(
        [query_weight, key_weight, value_weight, output_weight.T, inner_weight, outer_weight.T], axis=1
    )
    weights = lax.all_gather(packed, ("head", "dp"), axis=0, tiled=True).reshape(2, model, -1)
    wqkv = weights[:, :, : 3 * half]
    wo = weights[:, :, 3 * half : 4 * half]
    wi = weights[:, :, 4 * half : 4 * half + hid]
    wt = weights[:, :, 4 * half + hid :]

    small = jnp.concatenate(
        [query_up, value_up]
        + [b.astype(F32).reshape(-1, half) for b in (query_bias, value_bias, inner_bias)],
        axis=0,
    )
    other = lax.ppermute(small, "head", SWAP)
    both = jnp.where(me == 0, jnp.stack([small, other]), jnp.stack([other, small]))
    uq, uv = both[:, :rank], both[:, rank : 2 * rank]
    bq, bv = both[:, 2 * rank], both[:, 2 * rank + 1]
    bi = both[:, 2 * rank + 2 :].reshape(2, 1, hid)

    down = jnp.concatenate([query_down, value_down], axis=1)
    z = mm(tokens.reshape(-1, model), down).astype(BF16)
    zf = z.astype(F32).reshape(micro, slots, 2 * rank)
    exact = functools.partial(
        jnp.einsum, "mtr,hrc->mhtc", precision=lax.Precision.HIGHEST, preferred_element_type=F32
    )
    addq = scale * exact(zf[..., :rank], uq) + bq[None, :, None, :]
    addv = scale * exact(zf[..., rank:], uv) + bv[None, :, None, :]
    zt = z.reshape(micro, slots, 2 * rank).transpose(0, 2, 1)

    def split(a):
        high = a.astype(BF16)
        return high, (a - high.astype(F32)).astype(BF16)

    up = jnp.concatenate([*split(scale * uq), *split(scale * uv)], axis=1)
    down_t = jnp.concatenate([down.T, down.T], axis=0)
    zero = jnp.zeros((model,), F32)
    vec = jnp.stack(
        [
            a.astype(F32)
            for a in (output_bias, outer_bias, first_scale, first_bias, second_scale, second_bias, zero, zero)
        ]
    )

    order = jnp.argsort(-bucket)
    pairs = jnp.stack([order[jnp.array([0, 3])], order[jnp.array([1, 2])]]).astype(jnp.int32)
    ids, peer_ids = pairs[me], pairs[1 - me]
    where = jnp.concatenate([ids, peer_ids])

    qkv, probs, ctx = run_fwd(ids, bucket, tokens, wqkv, addq, addv, live)
    act, g1, gctx = run_mid(ids, tokens, ctx, cotangent, live, wo, wi, wt, bi, vec)
    peer_act = lax.ppermute(act, "head", SWAP)
    grad, lora = run_bwd(ids, bucket, qkv, probs, gctx, g1, wqkv, zt, up, down_t)
    peer_grad = lax.ppermute(grad, "head", SWAP)
    lora = jnp.sum(lora, axis=0)
    lora = jnp.concatenate([lora[:, :rank, :half], lora[:, rank:, 2 * half :]], axis=2)
    lora = jnp.where(me == 0, lora[0], lora[1]) + lax.ppermute(jnp.where(me == 0, lora[1], lora[0]), "head", SWAP)
    lora = lax.psum(lora, "dp")
    return place(where, act, peer_act), place(where, grad, peer_grad), lora[:, :half], lora[:, half:]


def solution(mesh):
    return jax.shard_map(
        shards,
        mesh=mesh,
        in_specs=(
            P(None, "dp", None), P(None, "dp"), P(),
            P("dp", "head"), P("dp", "head"), P("dp", "head"), P("head", "dp"), P("dp", "head"), P("head", "dp"),
            P("head"), P("head"), P(), P("head"), P(), P(), P(), P(), P(),
            P(), P(), P(None, "head"), P(None, "head"), P(None, "dp", None),
        ),
        out_specs=(P(None, "dp", None), P(None, "dp", None), P(None, "head"), P(None, "head")),
        check_vma=False,
    )
```

time: 760 us -> 568 us (0.75)
  Pallas kernels: 0 us -> 293 us
  matrix products: 215 us -> 12.1 us
  waiting for transfers between devices: 290 us -> 148 us
  blocking collectives: 146 us -> 58.9 us
  other arithmetic: 73.9 us -> 2.79 us
  local copies, waits for them, and re-layouts: 8.33 us -> 32.3 us
    pallas_call x0 -> x5, Pallas kernels: none -> 293 us  [the longest x2 194 us: place(): pl.pallas_call(place_kernel, out_shape=jax.ShapeDtypeStruct((2 * count, s...]
    psum x6 -> x0, waiting for transfers between devices: 265 us -> none  [the longest x2 111 us: shards(): lax.psum(plain_dot(context_low, cols_out).astype(jnp.bfloat16), 'head')]
    dot_general x104 -> x3, matrix products: 188 us -> 12.1 us  [the longest x1 4.57 us: shards(): addq = scale * exact(zf[..., :rank], uq) + bq[None, :, None, :]]
    all_gather x4 -> x0, blocking collectives: 85 us -> none  [the longest x1 24.8 us: collect(): lax.all_gather(key_weight, 'dp', axis=0, tiled=True)]
    ppermute x0 -> x4, waiting for transfers between devices: none -> 67.9 us  [the longest x1 67.9 us: shards(): lax.ppermute(jnp.where(me == 0, lora[1], lora[0]), 'head', SWAP)]
    all_gather x2 -> x1, waiting for transfers between devices: 24.2 us -> 79.7 us  [shards(): lax.all_gather(packed, ('head', 'dp'), axis=0, tiled=True)]
    sub x4 -> x0, matrix products: 27.1 us -> none  [shards(): expo = jnp.exp(scores - top_score)]
    reduce_sum x14 -> x1, other arithmetic: 23.6 us -> 0.02 us  [shards(): lora = jnp.sum(lora, axis=0)]
  transfers between devices with their start and end apart: 8 -> 5, of which waited for: 7 -> 2; matrix products, arithmetic and copies ran while one was open for 8% -> 4% of each run, Pallas kernels for 0% -> 17%
where the time goes in v1:
time: 568 us; the launch traced here: 567 us
  Pallas kernels  293 us (52%)
  waiting for transfers between devices  148 us (26%)
  blocking collectives  58.9 us (10%)
  local copies, waits for them, and re-layouts  32.3 us (6%)
  between operations  14.4 us (3%)
  matrix products  12.1 us (2%)
    pallas_call x2, Pallas kernels, place(): pl.pallas_call(place_kernel, out_shape=jax.ShapeDtypeStruct((2 * count, s...  194 us
    all_gather x1, waiting for transfers between devices, shards(): lax.all_gather(packed, ('head', 'dp'), axis=0, tiled=True)  79.7 us
    ppermute x1, waiting for transfers between devices, shards(): lax.ppermute(jnp.where(me == 0, lora[1], lora[0]), 'head', SWAP)  67.9 us
    psum x1, blocking collectives, shards(): lora = lax.psum(lora, 'dp')  58.9 us
    pallas_call x1, Pallas kernels, run_mid(): pl.pallas_call(mid_kernel, out_shape=(jax.ShapeDtypeStruct((n, slots, mod...  43.1 us
    pallas_call x1, Pallas kernels, run_bwd(): pl.pallas_call(bwd_kernel, out_shape=(jax.ShapeDtypeStruct((n, slots, mod...  30.1 us
    pallas_call x1, Pallas kernels, run_fwd(): pl.pallas_call(fwd_kernel, out_shape=(jax.ShapeDtypeStruct((n, 2, slots,...  26.1 us
  transfers between devices with their start and end apart: 5, of which 2 were waited for; matrix products, arithmetic and copies ran while one was open for 4% of the time, Pallas kernels for 17%

profile of v1, /device:TPU:0, one launch (start us, length us, event | category | flops | bytes accessed | tf_op | source)
XLA Modules:
  0.0 566.8 jit_solution(10523686049494138619)
XLA Ops:
  8.1 0.8 constant_dynamic-update-slice_fusion.2
  8.8 0.8 constant_dynamic-update-slice_fusion.1
  10.4 0.9 constant_dynamic-update-slice_fusion
  11.3 0.9 bitcast_dynamic-update-slice_fusion
  15.1 1.4 concatenate.23
  16.5 3.0 collective-permute-start
  24.4 2.9 convolution_convert_fusion
  27.5 1.4 copy.36.live_ref
  30.3 4.6 add_bitcast_fusion.1.addq_ref
  34.8 4.6 add_bitcast_fusion.addv_ref
  39.4 79.7 %all-gather.2.cloned.1.call-done = bf16[1536,4608]{1,0:T(8,128)(2,1)} async-done(((bf16[48,4608]{1,0:T(8,128)(2,1)}), bf16[1536,4608]{1,0:T(8,128)(2,1)}) %all-gather.2.cloned.1.call-update) | async-done | bytes 14155792 | tf_op jit(solution)/shard_map/all_gather | solution.py:371
  119.1 2.4 slice.81.wo_ref
  121.5 4.1 slice.74.w_ref
  125.6 7.9 %fusion.10 = (bf16[2,768,1536]{2,1,0:T(8,128)(2,1)}, bf16[2,768,1536]{2,1,0:T(8,128)(2,1)}) fusion(bf16[2,768,4608]{2,1,0:T(8,128)(2,1)} %bitcast.62), kind=kLoop, calls=%fused_computation.45 | loop fusion | bytes 18874368 | tf_op jit(solution)/shard_map/slice | solution.py:375
  133.5 26.1 %attention_forward.1 = (bf16[2,2,512,1152]{3,2,1,0:T(8,128)(2,1)}, bf16[2,2,6,512,512]{4,3,2,1,0:T(8,128)(2,1)}, bf16[2,512,768]{2,1,0:T(8,128)(2,1)S(1)}) custom-call(s32[2]{0:T(128)S(1)} %get-tuple-element.38.ids, s32[4]{0:T(128)S(1)} %copy-done.5, bf16[4,512,768]{2,1,0:T(8,128)(2,1)} %x_ref.3, bf16[2,768,1152]{2,1,0:T(8,128)(2,1)} %slice.74.w_ref, ...), custom_call_target="tpu_custom_call" | custom-call | tf_op jit(solution)/shard_map/attention_forward/pallas_call | solution.py:82
  159.6 1.1 copy-done.1
  160.7 43.1 %feed_forward.1 = (bf16[2,512,768]{2,1,0:T(8,128)(2,1)}, f32[2,512,768]{2,1,0:T(8,128)}, bf16[2,512,768]{2,1,0:T(8,128)(2,1)}) custom-call(s32[2]{0:T(128)} %copy-done.3, bf16[4,512,768]{2,1,0:T(8,128)(2,1)} %x_ref.3, bf16[2,512,768]{2,1,0:T(8,128)(2,1)} %copy-done.1, bf16[4,512,768]{2,1,0:T(8,128)(2,1)} %cot_ref.1, s32[4,512,1]{2,1,0:T(8,128)} %copy.36.live_ref, ...), custom_call_target="tpu_custom_call" | custom-call | tf_op jit(solution)/shard_map/feed_forward/pallas_call | solution.py:188
  203.9 1.4 copy-done
  205.3 30.1 %attention_backward.1 = (bf16[2,512,768]{2,1,0:T(8,128)(2,1)S(1)}, f32[2,2,16,1152]{3,2,1,0:T(8,128)S(1)}) custom-call(s32[2]{0:T(128)S(1)} %copy-done.4, s32[4]{0:T(128)S(1)} %copy-done.5, bf16[2,2,512,1152]{3,2,1,0:T(8,128)(2,1)} %get-tuple-element.16.qkv_ref, bf16[2,2,6,512,512]{4,3,2,1,0:T(8,128)(2,1)} %get-tuple-element.17.p_ref, ...), custom_call_target="tpu_custom_call" | custom-call | tf_op jit(solution)/shard_map/attention_backward/pallas_call | solution.py:291
  235.5 2.0 collective-permute-start.1
  238.3 67.9 %collective-permute-done.3 = f32[8,768]{1,0:T(8,128)S(1)} collective-permute-done((f32[8,768]{1,0:T(8,128)S(1)}, f32[8,768]{1,0:T(8,128)S(1)}, u32[]{:S(2)}, u32[]{:S(2)}) %collective-permute-start.3) | collective-permute-done | bytes 24608 | tf_op jit(solution)/shard_map/ppermute | solution.py:424
  306.2 58.9 %psum.7 = f32[8,768]{1,0:T(8,128)S(1)} all-reduce(f32[8,768]{1,0:T(8,128)S(1)} %bitcast_add_fusion), channel_id=1, replica_groups=mesh['dp'=16,'head'=2] {'dp'}, use_global_device_ids=true, to_apply=%region_2.3 | all-reduce | flops 6144 | bytes 49152 | tf_op jit(solution)/shard_map/psum | solution.py:425
  365.8 97.1 %place.3 = bf16[4,512,768]{2,1,0:T(8,128)(2,1)} custom-call(s32[4]{0:T(128)} %pad_add_fusion.1.ids, bf16[2,512,768]{2,1,0:T(8,128)(2,1)} %copy-done.2, bf16[2,512,768]{2,1,0:T(8,128)(2,1)} %collective-permute-done.2.peer_ref), custom_call_target="tpu_custom_call" | custom-call | tf_op jit(solution)/shard_map/place/pallas_call | solution.py:340
  462.9 97.1 %place.2 = bf16[4,512,768]{2,1,0:T(8,128)(2,1)} custom-call(s32[4]{0:T(128)} %pad_add_fusion.1.ids, bf16[2,512,768]{2,1,0:T(8,128)(2,1)} %get-tuple-element.15.own_ref, bf16[2,512,768]{2,1,0:T(8,128)(2,1)} %collective-permute-done.1.peer_ref), custom_call_target="tpu_custom_call" | custom-call | tf_op jit(solution)/shard_map/place/pallas_call | solution.py:340
  (73 shorter events, 12.2 us)
Async XLA Ops:
  7.2 20.2 %copy-start.8 = (bf16[768]{0:T(1024)(128)(2,1)S(1)}, bf16[768]{0:T(1024)(128)(2,1)}, u32[]{:S(2)}) copy-start(bf16[768]{0:T(1024)(128)(2,1)} %param.36) | copy-start | bytes 4612
  7.2 20.2 %copy-start.9 = (bf16[768]{0:T(1024)(128)(2,1)S(1)}, bf16[768]{0:T(1024)(128)(2,1)}, u32[]{:S(2)}) copy-start(bf16[768]{0:T(1024)(128)(2,1)} %param.38) | copy-start | bytes 4612
  7.2 20.2 %copy-start.10 = (bf16[768]{0:T(1024)(128)(2,1)S(1)}, bf16[768]{0:T(1024)(128)(2,1)}, u32[]{:S(2)}) copy-start(bf16[768]{0:T(1024)(128)(2,1)} %param.39) | copy-start | bytes 4612
  7.2 20.2 %copy-start.11 = (bf16[768]{0:T(1024)(128)(2,1)S(1)}, bf16[768]{0:T(1024)(128)(2,1)}, u32[]{:S(2)}) copy-start(bf16[768]{0:T(1024)(128)(2,1)} %param.40) | copy-start | bytes 4612
  7.2 20.2 %copy-start.12 = (bf16[768]{0:T(1024)(128)(2,1)S(1)}, bf16[768]{0:T(1024)(128)(2,1)}, u32[]{:S(2)}) copy-start(bf16[768]{0:T(1024)(128)(2,1)} %param.41) | copy-start | bytes 4612
  7.2 20.2 %copy-start.13 = (bf16[768]{0:T(1024)(128)(2,1)S(1)}, bf16[768]{0:T(1024)(128)(2,1)}, u32[]{:S(2)}) copy-start(bf16[768]{0:T(1024)(128)(2,1)} %param.42) | copy-start | bytes 4612
  7.2 20.3 %copy-start.7 = (s32[4,512]{1,0:T(4,128)S(1)}, s32[4,512]{1,0:T(4,128)}, u32[]{:S(2)}) copy-start(s32[4,512]{1,0:T(4,128)} %param.26) | copy-start | bytes 24580
  7.2 111.8 %all-gather.2.cloned.1.call-start = ((), (), s32[]{:S(2)}) async-start(), calls=%async_computation | async-start | bytes 14598144 | tf_op jit(solution)/shard_map/all_gather | solution.py:371
  12.2 0.8 copy-start.6
  16.5 13.0 %collective-permute-start = (f32[22,384]{1,0:T(8,128)S(1)}, f32[22,384]{1,0:T(8,128)S(1)}, u32[]{:S(2)}, u32[]{:S(2)}) collective-permute-start(f32[22,384]{1,0:T(8,128)S(1)} %concatenate.23), channel_id=1, source_target_pairs={{0,1},{1,0},{2,3},{3,2},{4,5},{5,4},{6,7},{7,6},{8,9},{9,8},{10,11... | collective-permute-start | bytes 101384 | tf_op jit(solution)/shard_map/ppermute | solution.py:382
  27.3 106.2 %copy-start.3 = (s32[2]{0:T(128)}, s32[2]{0:T(128)S(1)}, u32[]{:S(2)}) copy-start(s32[2]{0:T(128)S(1)} %get-tuple-element.38.ids) | copy-start | bytes 28
  125.6 7.9 %copy-start.5 = (s32[4]{0:T(128)S(1)}, s32[4]{0:T(128)}, u32[]{:S(2)}) copy-start(s32[4]{0:T(128)} %bucket.3) | copy-start | bytes 52
  159.6 1.1 copy-start.1
  160.7 43.2 %copy-start.4 = (s32[2]{0:T(128)S(1)}, s32[2]{0:T(128)}, u32[]{:S(2)}) copy-start(s32[2]{0:T(128)} %copy-done.3) | copy-start | bytes 28
  203.9 1.4 copy-start
  235.4 130.4 %copy-start.2 = (bf16[2,512,768]{2,1,0:T(8,128)(2,1)}, bf16[2,512,768]{2,1,0:T(8,128)(2,1)S(1)}, u32[]{:S(2)}) copy-start(bf16[2,512,768]{2,1,0:T(8,128)(2,1)S(1)} %get-tuple-element.20.own_ref) | copy-start | bytes 4718596
  235.4 130.4 %collective-permute-start.2 = (bf16[2,512,768]{2,1,0:T(8,128)(2,1)S(1)}, bf16[2,512,768]{2,1,0:T(8,128)(2,1)}, u32[]{:S(2)}, u32[]{:S(2)}) collective-permute-start(bf16[2,512,768]{2,1,0:T(8,128)(2,1)S(1)} %get-tuple-element.20.own_ref), channel_id=1, source_target_pairs={{0,1},{1,0},{2,3},{3,2},{4,5},{5,4},{6,7},{7,6},{8,9},{9,8},{10,11... | collective-permute-start | bytes 4718600 | tf_op jit(solution)/shard_map/ppermute | solution.py:421
  235.5 227.4 %collective-permute-start.1 = (bf16[2,512,768]{2,1,0:T(8,128)(2,1)}, bf16[2,512,768]{2,1,0:T(8,128)(2,1)}, u32[]{:S(2)}, u32[]{:S(2)}) collective-permute-start(bf16[2,512,768]{2,1,0:T(8,128)(2,1)} %get-tuple-element.15.own_ref), channel_id=1, source_target_pairs={{0,1},{1,0},{2,3},{3,2},{4,5},{5,4},{6,7},{7,6},{8,9},{9,8},{10,11... | collective-permute-start | bytes 4718600 | tf_op jit(solution)/shard_map/ppermute | solution.py:419
  237.5 68.7 %collective-permute-start.3 = (f32[8,768]{1,0:T(8,128)S(1)}, f32[8,768]{1,0:T(8,128)S(1)}, u32[]{:S(2)}, u32[]{:S(2)}) collective-permute-start(f32[8,768]{1,0:T(8,128)S(1)} %select_bitcast_fusion), channel_id=1, source_target_pairs={{0,1},{1,0},{2,3},{3,2},{4,5},{5,4},{6,7},{7,6},{8,9},{9,8},{10,11... | collective-permute-start | bytes 73736 | tf_op jit(solution)/shard_map/ppermute | solution.py:424
Sparse Core Ops, SparseCore 0:
  13.2 105.8 all-gather.1

commit v2 on v1

--- a/solution.py
+++ b/solution.py
@@ -1,5 +1,6 @@
 import functools
 import math
+
 import jax
 import jax.numpy as jnp
 from jax import lax
@@ -14,7 +15,10 @@
 NT = (((1,), (1,)), ((), ()))
 TN = (((0,), (0,)), ((), ()))
 NN = (((1,), (0,)), ((), ()))
-
+SWAP = [(0, 1), (1, 0)]
+RSQRT2 = 1.0 / math.sqrt(2.0)
+PHI0 = 1.0 / math.sqrt(2.0 * math.pi)
+ONCE = pl.Buffered(1)
 
 def mm(a, b, dims=NN):
     return lax.dot_general(a, b, dims, preferred_element_type=F32)
@@ -74,10 +78,10 @@
         attend(slots // 2)
 
 
-def run_fwd(ids, bucket, tokens, wqkv, addq, addv, live):
+def run_fwd(ids, bucket, tokens, weights, addq, addv, live):
     n = ids.shape[0]
     _, slots, model = tokens.shape
-    half = wqkv.shape[2] // 3
+    half = addq.shape[3]
     heads = half // 64
     return pl.pallas_call(
         fwd_kernel,
@@ -105,11 +109,7 @@
         ),
         compiler_params=pltpu.CompilerParams(vmem_limit_bytes=50 << 20),
         name="attention_forward",
-    )(ids, bucket, tokens, wqkv, addq, addv, live.reshape(live.shape[0], 1, slots))
-
-
-RSQRT2 = 1.0 / math.sqrt(2.0)
-PHI0 = 1.0 / math.sqrt(2.0 * math.pi)
+    )(ids, bucket, tokens, weights, addq, addv, live.reshape(live.shape[0], 1, slots))
 
 
 def gelu_parts(u):
@@ -130,106 +130,120 @@
     )
 
 
-def mid_kernel(
-    ids, x_ref, ctx_ref, cot_ref, live_ref, wo_ref, wi_ref, wt_ref, bi_ref, vec_ref,
-    act_ref, g1_ref, gctx_ref, slope, xhat, acc, low,
-):
-    slots, model = x_ref.shape[1], x_ref.shape[2]
-    half, hid = wo_ref.shape[2], wi_ref.shape[2]
-    step = 512
+def mid_kernel(ids, x_ref, ctx_ref, cot_ref, live_ref, w_hbm, bi_ref, vec_ref, *rest):
+    act_ref, full_ref, g1_ref, gctx_ref, wo, wi, wt, slope, xhat, acc, low, hidden, sems = rest[-13:]
+    model = x_ref.shape[2]
+    half, units = model // 2, wi.shape[1]
+    hid, step = units // 2, 768
+    copies = []
+    for k, (buf, start, cols) in enumerate(
+        ((wo, 3 * half, half), (wi, 4 * half, hid), (wt, 4 * half + hid, hid))
+    ):
+        for h in range(2):
+            copies.append(
+                pltpu.make_async_copy(
+                    w_hbm.at[h, :, start : start + cols],
+                    buf.at[:, h * cols : (h + 1) * cols],
+                    sems.at[2 * k + h],
+                )
+            )
+    for copy in copies:
+        copy.start()
     bo, b2 = vec_ref[0:1], vec_ref[1:2]
     s1, t1, s2, t2 = vec_ref[2:3], vec_ref[3:4], vec_ref[4:5], vec_ref[5:6]
-    r1 = x_ref[0].astype(F32) + bo
-    for h in range(2):
-        r1 = r1 + mm(ctx_ref[0, :, h * half : (h + 1) * half], wo_ref[h], NT)
-    xh, rstd1 = norm(r1)
+    for copy in copies[:2]:
+        copy.wait()
+    xh, rstd1 = norm(x_ref[0].astype(F32) + bo + mm(ctx_ref[0], wo[...], NT))
     xhat[...] = xh
-    normed = xh * s1 + t1
-    low[...] = normed.astype(BF16)
-    acc[...] = normed + b2
-    for h in range(2):
-
-        def up(j, _):
-            cols = pl.ds(pl.multiple_of(j * step, step), step)
-            u = mm(low[...], wi_ref[h, :, cols]) + bi_ref[h, :, cols]
-            a, d = gelu_parts(u)
-            slope[h, :, cols] = d
-            acc[...] += mm(a.astype(BF16), wt_ref[h, :, cols], NT)
-            return 0
-
-        lax.fori_loop(0, hid // step, up, 0)
-    xh2, rstd2 = norm(acc[...])
+    low[...] = (xh * s1 + t1).astype(BF16)
+    for copy in copies[2:]:
+        copy.wait()
+
+    def up(j, _):
+        cols = pl.ds(pl.multiple_of(j * step, step), step)
+        a, d = gelu_parts(mm(low[...], wi[:, cols]) + bi_ref[:, cols])
+        slope[:, cols] = d
+        hidden[:, cols] = a.astype(BF16)
+        return 0
+
+    lax.fori_loop(0, units // step, up, 0)
+    xh2, rstd2 = norm(mm(hidden[...], wt[...], NT) + (xhat[...] * s1 + t1) + b2)
     act_ref[0] = (xh2 * s2 + t2).astype(BF16)
-    e = cot_ref[0].astype(F32) * live_ref[0].astype(F32) * s2
-    g2 = norm_back(e, xh2, rstd2)
+    full_ref[0] = act_ref[0]
+    g2 = norm_back(cot_ref[0].astype(F32) * live_ref[0].astype(F32) * s2, xh2, rstd2)
     low[...] = g2.astype(BF16)
     acc[...] = g2
-    for h in range(2):
-
-        def down(j, _):
-            cols = pl.ds(pl.multiple_of(j * step, step), step)
-            g = mm(low[...], wt_ref[h, :, cols]) * slope[h, :, cols]
-            acc[...] += mm(g.astype(BF16), wi_ref[h, :, cols], NT)
-            return 0
-
-        lax.fori_loop(0, hid // step, down, 0)
-    g1 = norm_back(acc[...] * s1, xhat[...], rstd1)
+
+    def down(j, _):
+        cols = pl.ds(pl.multiple_of(j * step, step), step)
+        hidden[:, cols] = (mm(low[...], wt[:, cols]) * slope[:, cols]).astype(BF16)
+        return 0
+
+    lax.fori_loop(0, units // step, down, 0)
+    g1 = norm_back((acc[...] + mm(hidden[...], wi[...], NT)) * s1, xhat[...], rstd1)
     g1_ref[0] = g1
-    g1 = g1.astype(BF16)
-    for h in range(2):
-        gctx_ref[0, :, h * half : (h + 1) * half] = mm(g1, wo_ref[h]).astype(BF16)
-
-
-def run_mid(ids, tokens, ctx, cot, live, wo, wi, wt, bi, vec):
-    n = ids.shape[0]
-    _, slots, model = tokens.shape
-    half, hid = wo.shape[2], wi.shape[2]
-    one = pl.Buffered(1)
+    gctx_ref[0] = mm(g1.astype(BF16), wo[...]).astype(BF16)
+
+
+def run_mid(pos, ids, tokens, ctx, cot, live, weights, bi, vec, full):
+    micro, slots, model = tokens.shape
+    units = bi.shape[1]
+    own = lambda i, ids: (ids[pos], 0, 0)
+    same = lambda i, ids: (0, 0)
+    in_specs = [
+        pl.BlockSpec((1, slots, model), own),
+        pl.BlockSpec((1, slots, model), lambda i, ids: (pos, 0, 0)),
+        pl.BlockSpec((1, slots, model), own),
+        pl.BlockSpec((1, slots, 1), own),
+        pl.BlockSpec(memory_space=pl.ANY),
+        pl.BlockSpec((1, units), same, pipeline_mode=ONCE),
+        pl.BlockSpec((8, model), same, pipeline_mode=ONCE),
+    ]
+    args = [ids, tokens, ctx, cot, live.reshape(micro, slots, 1), weights, bi, vec]
+    aliases = {}
+    if full is not None:
+        in_specs.append(pl.BlockSpec(memory_space=pl.ANY))
+        args.append(full)
+        aliases = {8: 1}
+    first = pl.BlockSpec((1, slots, model), lambda i, ids: (0, 0, 0))
     return pl.pallas_call(
         mid_kernel,
         out_shape=(
-            jax.ShapeDtypeStruct((n, slots, model), BF16),
-            jax.ShapeDtypeStruct((n, slots, model), F32),
-            jax.ShapeDtypeStruct((n, slots, model), BF16),
+            jax.ShapeDtypeStruct((1, slots, model), BF16),
+            jax.ShapeDtypeStruct(tokens.shape, BF16),
+            jax.ShapeDtypeStruct((1, slots, model), F32),
+            jax.ShapeDtypeStruct((1, slots, model), BF16),
         ),
         grid_spec=pltpu.PrefetchScalarGridSpec(
             num_scalar_prefetch=1,
-            grid=(n,),
-            in_specs=[
-                pl.BlockSpec((1, slots, model), lambda i, ids: (ids[i], 0, 0)),
-                pl.BlockSpec((1, slots, model), lambda i, ids: (i, 0, 0)),
-                pl.BlockSpec((1, slots, model), lambda i, ids: (ids[i], 0, 0)),
-                pl.BlockSpec((1, slots, 1), lambda i, ids: (ids[i], 0, 0)),
-                pl.BlockSpec((2, model, half), lambda i, ids: (0, 0, 0), pipeline_mode=one),
-                pl.BlockSpec((2, model, hid), lambda i, ids: (0, 0, 0), pipeline_mode=one),
-                pl.BlockSpec((2, model, hid), lambda i, ids: (0, 0, 0), pipeline_mode=one),
-                pl.BlockSpec((2, 1, hid), lambda i, ids: (0, 0, 0), pipeline_mode=one),
-                pl.BlockSpec((8, model), lambda i, ids: (0, 0), pipeline_mode=one),
-            ],
-            out_specs=[
-                pl.BlockSpec((1, slots, model), lambda i, ids: (i, 0, 0)),
-                pl.BlockSpec((1, slots, model), lambda i, ids: (i, 0, 0)),
-                pl.BlockSpec((1, slots, model), lambda i, ids: (i, 0, 0)),
-            ],
+            grid=(1,),
+            in_specs=in_specs,
+            out_specs=[first, pl.BlockSpec((1, slots, model), own), first, first],
             scratch_shapes=[
-                pltpu.VMEM((2, slots, hid), F32),
+                pltpu.VMEM((model, model), BF16),
+                pltpu.VMEM((model, units), BF16),
+                pltpu.VMEM((model, units), BF16),
+                pltpu.VMEM((slots, units), F32),
                 pltpu.VMEM((slots, model), F32),
                 pltpu.VMEM((slots, model), F32),
                 pltpu.VMEM((slots, model), BF16),
+                pltpu.VMEM((slots, units), BF16),
+                pltpu.SemaphoreType.DMA((6,)),
             ],
         ),
+        input_output_aliases=aliases,
         compiler_params=pltpu.CompilerParams(vmem_limit_bytes=58 << 20),
         name="feed_forward",
-    )(ids, tokens, ctx, cot, live.reshape(live.shape[0], slots, 1), wo, wi, wt, bi, vec)
+    )(*args)
 
 
 def bwd_kernel(
-    ids, bucket, qkv_ref, p_ref, gctx_ref, g1_ref, w_ref, zt_ref, u_ref, d_ref,
-    grad_ref, lora_ref, dqkv, total, tlo,
+    pos, ids, bucket, qkv_ref, p_ref, gctx_ref, g1_ref, w_ref, zt_ref, u_ref, d_ref, *rest
 ):
+    grad_ref, full_ref, lora_ref, dqkv, total = rest[-5:]
     slots, width = gctx_ref.shape[1], gctx_ref.shape[2]
-    i, h = pl.program_id(0), pl.program_id(1)
-    span = bucket[ids[i]]
+    h = pl.program_id(1)
+    span = bucket[ids[pos]]
     masks = lane_masks()
 
     def attend(size):
@@ -282,76 +296,86 @@
     @pl.when(h == 1)
     def _():
         grad_ref[0] = (total[...] + part).astype(BF16)
-
-
-def run_bwd(ids, bucket, qkv, probs, gctx, g1, wqkv, zt, up, down):
-    n, _, slots, width3 = qkv.shape
+        full_ref[0] = grad_ref[0]
+
+
+def run_bwd(pos, ids, bucket, qkv, probs, gctx, g1, weights, zt, up, down, full):
+    _, _, slots, width3 = qkv.shape
+    micro = zt.shape[0]
     half, model = width3 // 3, g1.shape[2]
     heads = half // 64
+    in_specs = [
+        pl.BlockSpec((1, 1, slots, width3), lambda i, h, ids, b: (pos, h, 0, 0)),
+        pl.BlockSpec((1, 1, heads, slots, slots), lambda i, h, ids, b: (pos, h, 0, 0, 0)),
+        pl.BlockSpec((1, slots, half), lambda i, h, ids, b: (0, 0, h)),
+        pl.BlockSpec((1, slots, model), lambda i, h, ids, b: (0, 0, 0)),
+        pl.BlockSpec((1, model, width3), lambda i, h, ids, b: (h, 0, 0)),
+        pl.BlockSpec((1, 16, slots), lambda i, h, ids, b: (ids[pos], 0, 0)),
+        pl.BlockSpec((1, 32, half), lambda i, h, ids, b: (h, 0, 0)),
+        pl.BlockSpec((32, model), lambda i, h, ids, b: (0, 0)),
+    ]
+    args = [ids, bucket, qkv, probs, gctx, g1, weights, zt, up, down]
+    aliases = {}
+    if full is not None:
+        in_specs.append(pl.BlockSpec(memory_space=pl.ANY))
+        args.append(full)
+        aliases = {10: 1}
     return pl.pallas_call(
-        bwd_kernel,
+        functools.partial(bwd_kernel, pos),
         out_shape=(
-            jax.ShapeDtypeStruct((n, slots, model), BF16),
-            jax.ShapeDtypeStruct((n, 2, 16, width3), F32),
+            jax.ShapeDtypeStruct((1, slots, model), BF16),
+            jax.ShapeDtypeStruct((micro, slots, model), BF16),
+            jax.ShapeDtypeStruct((1, 2, 16, width3), F32),
         ),
         grid_spec=pltpu.PrefetchScalarGridSpec(
             num_scalar_prefetch=2,
-            grid=(n, 2),
-            in_specs=[
-                pl.BlockSpec((1, 1, slots, width3), lambda i, h, ids, b: (i, h, 0, 0)),
-                pl.BlockSpec((1, 1, heads, slots, slots), lambda i, h, ids, b: (i, h, 0, 0, 0)),
-                pl.BlockSpec((1, slots, half), lambda i, h, ids, b: (i, 0, h)),
-                pl.BlockSpec((1, slots, model), lambda i, h, ids, b: (i, 0, 0)),
-                pl.BlockSpec((1, model, width3), lambda i, h, ids, b: (h, 0, 0)),
-                pl.BlockSpec((1, 16, slots), lambda i, h, ids, b: (ids[i], 0, 0)),
-                pl.BlockSpec((1, 32, half), lambda i, h, ids, b: (h, 0, 0)),
-                pl.BlockSpec((32, model), lambda i, h, ids, b: (0, 0)),
+            grid=(1, 2),
+            in_specs=in_specs,
+            out_specs=[
+                pl.BlockSpec((1, slots, model), lambda i, h, ids, b: (0, 0, 0)),
+                pl.BlockSpec((1, slots, model), lambda i, h, ids, b: (ids[pos], 0, 0)),
+                pl.BlockSpec((1, 1, 16, width3), lambda i, h, ids, b: (0, h, 0, 0)),
             ],
-            out_specs=[
-                pl.BlockSpec((1, slots, model), lambda i, h, ids, b: (i, 0, 0)),
-                pl.BlockSpec((1, 1, 16, width3), lambda i, h, ids, b: (i, h, 0, 0)),
-            ],
-            scratch_shapes=[
-                pltpu.VMEM((slots, width3), BF16),
-                pltpu.VMEM((slots, model), F32),
-                pltpu.VMEM((8, 128), F32),
-            ],
-        ),
+            scratch_shapes=[pltpu.VMEM((slots, width3), BF16), pltpu.VMEM((slots, model), F32)],
+        ),
+        input_output_aliases=aliases,
         compiler_params=pltpu.CompilerParams(vmem_limit_bytes=50 << 20),
         name="attention_backward",
-    )(ids, bucket, qkv, probs, gctx, g1, wqkv, zt, up, down)
-
-
-def place_kernel(ids, own_ref, peer_ref, out_ref, sems):
-    count = own_ref.shape[0]
-    copies = [
-        pltpu.make_async_copy(ref.at[i], out_ref.at[ids[k * count + i]], sems.at[k * count + i])
-        for k, ref in enumerate((own_ref, peer_ref))
-        for i in range(count)
-    ]
-    for copy in copies:
-        copy.start()
-    for copy in copies:
-        copy.wait()
-
-
-def place(ids, own, peer):
-    count, slots, model = own.shape
+    )(*args)
+
+
+def place_kernel(ids, full_ref, piece_ref, out_ref):
+    out_ref[...] = piece_ref[...]
+
+
+def place(pos, ids, full, piece):
+    _, slots, model = full.shape
     return pl.pallas_call(
         place_kernel,
-        out_shape=jax.ShapeDtypeStruct((2 * count, slots, model), own.dtype),
+        out_shape=jax.ShapeDtypeStruct(full.shape, full.dtype),
         grid_spec=pltpu.PrefetchScalarGridSpec(
             num_scalar_prefetch=1,
-            grid=(),
-            in_specs=[pl.BlockSpec(memory_space=pl.ANY)] * 2,
-            out_specs=pl.BlockSpec(memory_space=pl.ANY),
-            scratch_shapes=[pltpu.SemaphoreType.DMA((2 * count,))],
-        ),
+            grid=(2,),
+            in_specs=[
+                pl.BlockSpec(memory_space=pl.ANY),
+                pl.BlockSpec((1, slots // 2, model), lambda i, ids: (0, i, 0)),
+            ],
+            out_specs=pl.BlockSpec((1, slots // 2, model), lambda i, ids: (ids[pos], i, 0)),
+        ),
+        input_output_aliases={1: 0},
         name="place",
-    )(ids, own, peer)
-
-
-SWAP = [(0, 1), (1, 0)]
+    )(ids, full, piece)
+
+
+def sum_over_dp(a):
+    size = lax.axis_size("dp")
+    if size & (size - 1):
+        return lax.psum(a, "dp")
+    bit = 1
+    while bit < size:
+        a = a + lax.ppermute(a, "dp", [(i, i ^ bit) for i in range(size)])
+        bit *= 2
+    return a
 
 
 def shards(
@@ -369,10 +393,6 @@
         [query_weight, key_weight, value_weight, output_weight.T, inner_weight, outer_weight.T], axis=1
     )
     weights = lax.all_gather(packed, ("head", "dp"), axis=0, tiled=True).reshape(2, model, -1)
-    wqkv = weights[:, :, : 3 * half]
-    wo = weights[:, :, 3 * half : 4 * half]
-    wi = weights[:, :, 4 * half : 4 * half + hid]
-    wt = weights[:, :, 4 * half + hid :]
 
     small = jnp.concatenate(
         [query_up, value_up]
@@ -383,7 +403,7 @@
     both = jnp.where(me == 0, jnp.stack([small, other]), jnp.stack([other, small]))
     uq, uv = both[:, :rank], both[:, rank : 2 * rank]
     bq, bv = both[:, 2 * rank], both[:, 2 * rank + 1]
-    bi = both[:, 2 * rank + 2 :].reshape(2, 1, hid)
+    bi = both[:, 2 * rank + 2 :].reshape(1, 2 * hid)
 
     down = jnp.concatenate([query_down, value_down], axis=1)
     z = mm(tokens.reshape(-1, model), down).astype(BF16)
@@ -412,18 +432,23 @@
     order = jnp.argsort(-bucket)
     pairs = jnp.stack([order[jnp.array([0, 3])], order[jnp.array([1, 2])]]).astype(jnp.int32)
     ids, peer_ids = pairs[me], pairs[1 - me]
-    where = jnp.concatenate([ids, peer_ids])
-
-    qkv, probs, ctx = run_fwd(ids, bucket, tokens, wqkv, addq, addv, live)
-    act, g1, gctx = run_mid(ids, tokens, ctx, cotangent, live, wo, wi, wt, bi, vec)
-    peer_act = lax.ppermute(act, "head", SWAP)
-    grad, lora = run_bwd(ids, bucket, qkv, probs, gctx, g1, wqkv, zt, up, down_t)
-    peer_grad = lax.ppermute(grad, "head", SWAP)
-    lora = jnp.sum(lora, axis=0)
+
+    qkv, probs, ctx = run_fwd(ids, bucket, tokens, weights, addq, addv, live)
+    acts = grads = lora = None
+    from_peer = []
+    for pos in range(2):
+        act, acts, g1, gctx = run_mid(pos, ids, tokens, ctx, cotangent, live, weights, bi, vec, acts)
+        peer_act = lax.ppermute(act, "head", SWAP)
+        grad, grads, part = run_bwd(pos, ids, bucket, qkv, probs, gctx, g1, weights, zt, up, down_t, grads)
+        peer_grad = lax.ppermute(grad, "head", SWAP)
+        lora = part[0] if lora is None else lora + part[0]
+        from_peer.append((peer_act, peer_grad))
     lora = jnp.concatenate([lora[:, :rank, :half], lora[:, rank:, 2 * half :]], axis=2)
-    lora = jnp.where(me == 0, lora[0], lora[1]) + lax.ppermute(jnp.where(me == 0, lora[1], lora[0]), "head", SWAP)
-    lora = lax.psum(lora, "dp")
-    return place(where, act, peer_act), place(where, grad, peer_grad), lora[:, :half], lora[:, half:]
+    mine, other = jnp.where(me == 0, lora, lora[::-1])
+    lora = sum_over_dp(mine + lax.ppermute(other, "head", SWAP))
+    for pos, (peer_act, peer_grad) in enumerate(from_peer):
+        acts, grads = place(pos, peer_ids, acts, peer_act), place(pos, peer_ids, grads, peer_grad)
+    return acts, grads, lora[:, :half], lora[:, half:]
 
 
 def solution(mesh):

time: 568 us -> 300 us (0.53)
  Pallas kernels: 293 us -> 120 us
  blocking collectives: 58.9 us -> 0 us
  waiting for transfers between devices: 148 us -> 121 us
  local copies, waits for them, and re-layouts: 32.3 us -> 18.7 us
    pallas_call x4 -> x8, Pallas kernels: 267 us -> 93.6 us  [the longest x2 48.3 us: run_mid(): pl.pallas_call(mid_kernel, out_shape=(jax.ShapeDtypeStruct((1, slots, mod...]
    psum x1 -> x0, blocking collectives: 58.9 us -> none  [shards(): lora = lax.psum(lora, 'dp')]
    ppermute x1 -> x5, waiting for transfers between devices: 67.9 us -> 42.1 us  [the longest x1 31.8 us: shards(): lora = sum_over_dp(mine + lax.ppermute(other, 'head', SWAP))]
    slice x5 -> x2, local copies, waits for them, and re-layouts: 15 us -> 0.61 us  [the longest x1 0.61 us: shards(): return (acts, grads, lora[:, :half], lora[:, half:])]
  transfers between devices with their start and end apart: 5 -> 11, of which waited for: 2 -> 6; matrix products, arithmetic and copies ran while one was open for 4% -> 8% of each run, Pallas kernels for 17% -> 14%
where the time goes in v2:
time: 300 us; the launch traced here: 299 us
  waiting for transfers between devices  121 us (40%)
  Pallas kernels  120 us (40%)
  local copies, waits for them, and re-layouts  18.7 us (6%)
  between operations  14.4 us (5%)
  matrix products  12.1 us (4%)
  starting transfers between devices  10.7 us (4%)
    all_gather x1, waiting for transfers between devices, shards(): lax.all_gather(packed, ('head', 'dp'), axis=0, tiled=True)  79.1 us
    pallas_call x2, Pallas kernels, run_mid(): pl.pallas_call(mid_kernel, out_shape=(jax.ShapeDtypeStruct((1, slots, mod...  48.3 us
    pallas_call x2, Pallas kernels, run_bwd(): pl.pallas_call(functools.partial(bwd_kernel, pos), out_shape=(jax.ShapeDt...  35 us
    ppermute x1, waiting for transfers between devices, shards(): lora = sum_over_dp(mine + lax.ppermute(other, 'head', SWAP))  31.8 us
    pallas_call x1, Pallas kernels, run_fwd(): pl.pallas_call(fwd_kernel, out_shape=(jax.ShapeDtypeStruct((n, 2, slots,...  26.1 us
    ppermute x4, waiting for transfers between devices, sum_over_dp(): a = a + lax.ppermute(a, 'dp', [(i, i ^ bit) for i in range(size)])  10.3 us
    pallas_call x4, Pallas kernels, place(): pl.pallas_call(place_kernel, out_shape=jax.ShapeDtypeStruct(full.shape, f...  10.3 us
    unnamed x43, local copies, waits for them, and re-layouts  8.43 us
  transfers between devices with their start and end apart: 11, of which 6 were waited for; matrix products, arithmetic and copies ran while one was open for 8% of the time, Pallas kernels for 14%

profile of v2, /device:TPU:0, one launch (start us, length us, event | category | flops | bytes accessed | tf_op | source)
XLA Modules:
  0.0 299.1 jit_solution(17152023703301814685)
XLA Ops:
  15.0 1.4 concatenate.19
  16.5 3.0 %collective-permute-start = (f32[22,384]{1,0:T(8,128)S(1)}, f32[22,384]{1,0:T(8,128)S(1)}, u32[]{:S(2)}, u32[]{:S(2)}) collective-permute-start(f32[22,384]{1,0:T(8,128)S(1)} %concatenate.19), channel_id=1, source_target_pairs={{0,1},{1,0},{2,3},{3,2},{4,5},{5,4},{6,7},{7,6},{8,9},{9,8},{10,11... | collective-permute-start | bytes 101384 | tf_op jit(solution)/shard_map/ppermute | solution.py:402
  24.3 2.9 convolution_convert_fusion
  27.9 1.3 copy.42.live_ref
  30.7 4.7 %add_bitcast_fusion.1.addq_ref = f32[4,2,512,384]{3,2,1,0:T(8,128)} fusion(f32[2,384]{1,0:T(2,128)S(1)} %get-tuple-element.59, bf16[4,512,16]{1,2,0:T(8,128)(2,1)S(1)} %bitcast.60, f32[2,22,384]{2,1,0:T(8,128)S(1)} %maximum_select_fusion), kind=kOutput, calls=%fused_computation.3 | convolution fusion | flops 154140672 | bytes 6351872 | tf_op jit(solution)/shard_map/mtr,hrc->mhtc/dot_general | solution.py:414
  35.3 4.5 %add_bitcast_fusion.addv_ref = f32[4,2,512,384]{3,2,1,0:T(8,128)} fusion(f32[2,384]{1,0:T(2,128)S(1)} %get-tuple-element.58, bf16[4,512,16]{1,2,0:T(8,128)(2,1)S(1)} %bitcast.61, f32[2,22,384]{2,1,0:T(8,128)S(1)} %maximum_select_fusion), kind=kOutput, calls=%fused_computation.2 | convolution fusion | flops 154140672 | bytes 6351872 | tf_op jit(solution)/shard_map/mtr,hrc->mhtc/dot_general | solution.py:415
  39.9 79.1 %all-gather.2.cloned.1.call-done = bf16[1536,4608]{1,0:T(8,128)(2,1)} async-done(((bf16[48,4608]{1,0:T(8,128)(2,1)}), bf16[1536,4608]{1,0:T(8,128)(2,1)}) %all-gather.2.cloned.1.call-update) | async-done | bytes 14155792 | tf_op jit(solution)/shard_map/all_gather | solution.py:395
  119.0 26.1 %attention_forward.1 = (bf16[2,2,512,1152]{3,2,1,0:T(8,128)(2,1)}, bf16[2,2,6,512,512]{4,3,2,1,0:T(8,128)(2,1)}, bf16[2,512,768]{2,1,0:T(8,128)(2,1)S(1)}) custom-call(s32[2]{0:T(128)S(1)} %get-tuple-element.54.ids, s32[4]{0:T(128)S(1)} %copy-done.7, bf16[4,512,768]{2,1,0:T(8,128)(2,1)} %x_ref.5, bf16[2,768,4608]{2,1,0:T(8,128)(2,1)} %bitcast.64, ...), custom_call_target="tpu_custom_call" | custom-call | tf_op jit(solution)/shard_map/attention_forward/pallas_call | solution.py:86
  146.3 24.0 %feed_forward.2 = (bf16[1,512,768]{2,1,0:T(8,128)(2,1)}, bf16[4,512,768]{2,1,0:T(8,128)(2,1)}, f32[1,512,768]{2,1,0:T(8,128)}, bf16[1,512,768]{2,1,0:T(8,128)(2,1)}) custom-call(s32[2]{0:T(128)} %copy-done.5, bf16[4,512,768]{2,1,0:T(8,128)(2,1)} %x_ref.5, bf16[2,512,768]{2,1,0:T(8,128)(2,1)} %copy-done, bf16[4,512,768]{2,1,0:T(8,128)(2,1)} %cot_ref.3, ...), custom_call_target="tpu_custom_call" | custom-call | tf_op jit(solution)/shard_map/feed_forward/pallas_call | solution.py:209
  170.4 24.2 %feed_forward.3 = (bf16[1,512,768]{2,1,0:T(8,128)(2,1)}, bf16[4,512,768]{2,1,0:T(8,128)(2,1)}, f32[1,512,768]{2,1,0:T(8,128)}, bf16[1,512,768]{2,1,0:T(8,128)(2,1)}) custom-call(s32[2]{0:T(128)} %copy-done.5, bf16[4,512,768]{2,1,0:T(8,128)(2,1)} %x_ref.5, bf16[2,512,768]{2,1,0:T(8,128)(2,1)} %copy-done, ...), custom_call_target="tpu_custom_call", output_to_operand_aliasing={{1}: (8, {})} | custom-call | tf_op jit(solution)/shard_map/feed_forward/pallas_call | solution.py:209
  194.7 2.0 collective-permute-start.2
  196.8 19.1 %attention_backward.2 = (bf16[1,512,768]{2,1,0:T(8,128)(2,1)S(1)}, bf16[4,512,768]{2,1,0:T(8,128)(2,1)}, f32[1,2,16,1152]{3,2,1,0:T(8,128)S(1)}) custom-call(s32[2]{0:T(128)S(1)} %copy-done.6, s32[4]{0:T(128)S(1)} %copy-done.7, bf16[2,2,512,1152]{3,2,1,0:T(8,128)(2,1)} %get-tuple-element.28.qkv_ref, bf16[2,2,6,512,512]{4,3,2,1,0:T(8,128)(2,1)} %get-tuple-element.29.p_ref, ...), custom_call_target="tpu_custom_call" | custom-call | tf_op jit(solution)/shard_map/attention_backward/pallas_call | solution.py:323
  215.8 15.9 %attention_backward.3 = (bf16[1,512,768]{2,1,0:T(8,128)(2,1)S(1)}, bf16[4,512,768]{2,1,0:T(8,128)(2,1)}, f32[1,2,16,1152]{3,2,1,0:T(8,128)S(1)}) custom-call(s32[2]{0:T(128)S(1)} %copy-done.6, s32[4]{0:T(128)S(1)} %copy-done.7, bf16[2,2,512,1152]{3,2,1,0:T(8,128)(2,1)} %get-tuple-element.28.qkv_ref, ...), custom_call_target="tpu_custom_call", output_to_operand_aliasing={{1}: (10, {})} | custom-call | tf_op jit(solution)/shard_map/attention_backward/pallas_call | solution.py:323
  231.8 2.0 collective-permute-start.4
  233.9 31.8 %collective-permute-done.5 = f32[8,768]{1,0:T(8,128)S(1)} collective-permute-done((f32[8,768]{1,0:T(8,128)S(1)}, f32[8,768]{1,0:T(8,128)S(1)}, u32[]{:S(2)}, u32[]{:S(2)}) %collective-permute-start.5) | collective-permute-done | bytes 24608 | tf_op jit(solution)/shard_map/ppermute | solution.py:448
  266.9 1.4 collective-permute-start.7
  268.3 2.4 collective-permute-done.7
  271.4 3.2 %collective-permute-done.8 = f32[8,768]{1,0:T(8,128)S(1)} collective-permute-done((f32[8,768]{1,0:T(8,128)S(1)}, f32[8,768]{1,0:T(8,128)S(1)}, u32[]{:S(2)}, u32[]{:S(2)}) %collective-permute-start.8) | collective-permute-done | bytes 24608 | tf_op jit(solution)/shard_map/ppermute | solution.py:376
  274.6 1.5 collective-permute-start.9
  276.0 3.5 %collective-permute-done.9 = f32[8,768]{1,0:T(8,128)S(1)} collective-permute-done((f32[8,768]{1,0:T(8,128)S(1)}, f32[8,768]{1,0:T(8,128)S(1)}, u32[]{:S(2)}, u32[]{:S(2)}) %collective-permute-start.9) | collective-permute-done | bytes 24608 | tf_op jit(solution)/shard_map/ppermute | solution.py:376
  281.1 2.6 place.4.full_ref
  284.6 2.6 place.5
  287.1 2.6 place.6.full_ref
  289.7 2.6 place.7
  (98 shorter events, 20.2 us)
Async XLA Ops:
  7.2 20.7 %copy-start.11 = (s32[4,512]{1,0:T(4,128)S(1)}, s32[4,512]{1,0:T(4,128)}, u32[]{:S(2)}) copy-start(s32[4,512]{1,0:T(4,128)} %param.26) | copy-start | bytes 24580
  7.2 111.8 %all-gather.2.cloned.1.call-start = ((), (), s32[]{:S(2)}) async-start(), calls=%async_computation | async-start | bytes 14598144 | tf_op jit(solution)/shard_map/all_gather | solution.py:395
  12.2 17.0 %copy-start.12 = (bf16[768]{0:T(1024)(128)(2,1)S(1)}, bf16[768]{0:T(1024)(128)(2,1)}, u32[]{:S(2)}) copy-start(bf16[768]{0:T(1024)(128)(2,1)} %param.36) | copy-start | bytes 4612
  12.2 17.0 %copy-start.14 = (bf16[768]{0:T(1024)(128)(2,1)S(1)}, bf16[768]{0:T(1024)(128)(2,1)}, u32[]{:S(2)}) copy-start(bf16[768]{0:T(1024)(128)(2,1)} %param.39) | copy-start | bytes 4612
  12.2 17.0 %copy-start.15 = (bf16[768]{0:T(1024)(128)(2,1)S(1)}, bf16[768]{0:T(1024)(128)(2,1)}, u32[]{:S(2)}) copy-start(bf16[768]{0:T(1024)(128)(2,1)} %param.40) | copy-start | bytes 4612
  12.2 17.0 %copy-start.16 = (bf16[768]{0:T(1024)(128)(2,1)S(1)}, bf16[768]{0:T(1024)(128)(2,1)}, u32[]{:S(2)}) copy-start(bf16[768]{0:T(1024)(128)(2,1)} %param.41) | copy-start | bytes 4612
  12.3 17.0 %copy-start.17 = (bf16[768]{0:T(1024)(128)(2,1)S(1)}, bf16[768]{0:T(1024)(128)(2,1)}, u32[]{:S(2)}) copy-start(bf16[768]{0:T(1024)(128)(2,1)} %param.42) | copy-start | bytes 4612
  16.5 13.5 %collective-permute-start = (f32[22,384]{1,0:T(8,128)S(1)}, f32[22,384]{1,0:T(8,128)S(1)}, u32[]{:S(2)}, u32[]{:S(2)}) collective-permute-start(f32[22,384]{1,0:T(8,128)S(1)} %concatenate.19), channel_id=1, source_target_pairs={{0,1},{1,0},{2,3},{3,2},{4,5},{5,4},{6,7},{7,6},{8,9},{9,8},{10,11... | collective-permute-start | bytes 101384 | tf_op jit(solution)/shard_map/ppermute | solution.py:402
  27.9 91.2 %copy-start.5 = (s32[2]{0:T(128)}, s32[2]{0:T(128)S(1)}, u32[]{:S(2)}) copy-start(s32[2]{0:T(128)S(1)} %get-tuple-element.54.ids) | copy-start | bytes 28
  35.3 83.7 %copy-start.7 = (s32[4]{0:T(128)S(1)}, s32[4]{0:T(128)}, u32[]{:S(2)}) copy-start(s32[4]{0:T(128)} %bucket.5) | copy-start | bytes 52
  170.4 26.4 %copy-start.2 = (f32[1,512,768]{2,1,0:T(8,128)S(1)}, f32[1,512,768]{2,1,0:T(8,128)}, u32[]{:S(2)}) copy-start(f32[1,512,768]{2,1,0:T(8,128)} %get-tuple-element.33.g1_ref) | copy-start | bytes 4718596
  170.4 26.4 %copy-start.4 = (bf16[1,512,768]{2,1,0:T(8,128)(2,1)S(1)}, bf16[1,512,768]{2,1,0:T(8,128)(2,1)}, u32[]{:S(2)}) copy-start(bf16[1,512,768]{2,1,0:T(8,128)(2,1)} %get-tuple-element.32.gctx_ref) | copy-start | bytes 2359300
  170.4 26.4 %copy-start.6 = (s32[2]{0:T(128)S(1)}, s32[2]{0:T(128)}, u32[]{:S(2)}) copy-start(s32[2]{0:T(128)} %copy-done.5) | copy-start | bytes 28
  194.6 85.5 %collective-permute-start.1 = (bf16[1,512,768]{2,1,0:T(8,128)(2,1)}, bf16[1,512,768]{2,1,0:T(8,128)(2,1)S(1)}, u32[]{:S(2)}, u32[]{:S(2)}) collective-permute-start(bf16[1,512,768]{2,1,0:T(8,128)(2,1)} %get-tuple-element.26), channel_id=1, source_target_pairs={{0,1},{1,0},{2,3},{3,2},{4,5},{5,4},{6,7},{7,6},{8,9},{9,8},{10,11... | collective-permute-start | bytes 2359304 | tf_op jit(solution)/shard_map/ppermute | solution.py:441
  194.7 88.9 %collective-permute-start.2 = (bf16[1,512,768]{2,1,0:T(8,128)(2,1)}, bf16[1,512,768]{2,1,0:T(8,128)(2,1)S(1)}, u32[]{:S(2)}, u32[]{:S(2)}) collective-permute-start(bf16[1,512,768]{2,1,0:T(8,128)(2,1)} %get-tuple-element.27), channel_id=1, source_target_pairs={{0,1},{1,0},{2,3},{3,2},{4,5},{5,4},{6,7},{7,6},{8,9},{9,8},{10,11... | collective-permute-start | bytes 2359304 | tf_op jit(solution)/shard_map/ppermute | solution.py:441
  196.7 19.1 %copy-start.1 = (f32[1,512,768]{2,1,0:T(8,128)S(1)}, f32[1,512,768]{2,1,0:T(8,128)}, u32[]{:S(2)}) copy-start(f32[1,512,768]{2,1,0:T(8,128)} %get-tuple-element.31.g1_ref) | copy-start | bytes 4718596
  196.8 19.1 %copy-start.3 = (bf16[1,512,768]{2,1,0:T(8,128)(2,1)S(1)}, bf16[1,512,768]{2,1,0:T(8,128)(2,1)}, u32[]{:S(2)}) copy-start(bf16[1,512,768]{2,1,0:T(8,128)(2,1)} %get-tuple-element.30.gctx_ref) | copy-start | bytes 2359300
  215.8 71.3 %collective-permute-start.3 = (bf16[1,512,768]{2,1,0:T(8,128)(2,1)S(1)}, bf16[1,512,768]{2,1,0:T(8,128)(2,1)}, u32[]{:S(2)}, u32[]{:S(2)}) collective-permute-start(bf16[1,512,768]{2,1,0:T(8,128)(2,1)S(1)} %get-tuple-element.36), channel_id=1, source_target_pairs={{0,1},{1,0},{2,3},{3,2},{4,5},{5,4},{6,7},{7,6},{8,9},{9,8},{10,11... | collective-permute-start | bytes 2359304 | tf_op jit(solution)/shard_map/ppermute | solution.py:443
  231.8 57.9 %collective-permute-start.4 = (bf16[1,512,768]{2,1,0:T(8,128)(2,1)S(1)}, bf16[1,512,768]{2,1,0:T(8,128)(2,1)}, u32[]{:S(2)}, u32[]{:S(2)}) collective-permute-start(bf16[1,512,768]{2,1,0:T(8,128)(2,1)S(1)} %get-tuple-element.37), channel_id=1, source_target_pairs={{0,1},{1,0},{2,3},{3,2},{4,5},{5,4},{6,7},{7,6},{8,9},{9,8},{10,11... | collective-permute-start | bytes 2359304 | tf_op jit(solution)/shard_map/ppermute | solution.py:443
  233.8 31.9 %collective-permute-start.5 = (f32[8,768]{1,0:T(8,128)S(1)}, f32[8,768]{1,0:T(8,128)S(1)}, u32[]{:S(2)}, u32[]{:S(2)}) collective-permute-start(f32[8,768]{1,0:T(8,128)S(1)} %slice_bitcast_fusion.4), channel_id=1, source_target_pairs={{0,1},{1,0},{2,3},{3,2},{4,5},{5,4},{6,7},{7,6},{8,9},{9,8},{10,11... | collective-permute-start | bytes 73736 | tf_op jit(solution)/shard_map/ppermute | solution.py:448
  265.7 1.2 collective-permute-start.6
  266.9 3.8 %collective-permute-start.7 = (f32[8,768]{1,0:T(8,128)S(1)}, f32[8,768]{1,0:T(8,128)S(1)}, u32[]{:S(2)}, u32[]{:S(2)}) collective-permute-start(f32[8,768]{1,0:T(8,128)S(1)} %add.73), channel_id=1, source_target_pairs={{0,4},{2,6},{4,0},{6,2},{8,12},{10,14},{12,8},{14,10},{16,20},{18,... | collective-permute-start | bytes 73736 | tf_op jit(solution)/shard_map/ppermute | solution.py:376
  270.8 3.8 %collective-permute-start.8 = (f32[8,768]{1,0:T(8,128)S(1)}, f32[8,768]{1,0:T(8,128)S(1)}, u32[]{:S(2)}, u32[]{:S(2)}) collective-permute-start(f32[8,768]{1,0:T(8,128)S(1)} %add.74), channel_id=1, source_target_pairs={{0,8},{2,10},{4,12},{6,14},{8,0},{10,2},{12,4},{14,6},{16,24},{18,... | collective-permute-start | bytes 73736 | tf_op jit(solution)/shard_map/ppermute | solution.py:376
  274.6 5.0 %collective-permute-start.9 = (f32[8,768]{1,0:T(8,128)S(1)}, f32[8,768]{1,0:T(8,128)S(1)}, u32[]{:S(2)}, u32[]{:S(2)}) collective-permute-start(f32[8,768]{1,0:T(8,128)S(1)} %add.75), channel_id=1, source_target_pairs={{0,16},{2,18},{4,20},{6,22},{8,24},{10,26},{12,28},{14,30},{16,0},... | collective-permute-start | bytes 73736 | tf_op jit(solution)/shard_map/ppermute | solution.py:376
  (5 other events, 20.7 us)
Sparse Core Ops, SparseCore 0:
  13.1 105.8 all-gather.1
